TPU v7x, 256 devices: a whole 4x4x8 slice. The times are simulated.
256 devices in a mesh: sector: 8 (over x, core), section: 32 (over z, y).
Axes of the slice: x: 4, y: 4, z: 8, core: 2. Of those that a mesh axis runs over, the one named last changes fastest.
Arguments:
- vectors: bfloat16 [98304, 512], P(('sector', 'section')), may hold values from -6 to 6
- sectors: int32 [98304, 2], P(('sector', 'section')), may hold values from 0 to 31, all different within a row; in each aligned block of 384 rows (0 to 383, 384 to 767, ...) at most 36 rows name the same one
- outcomes: int32 [98304, 2], P(('sector', 'section')), may hold values from 0 to 3
- sites: bfloat16 [2, 32, 512, 2048], P(None, 'sector'), may hold values from -0.25 to 0.25
- environments: bfloat16 [2, 32, 4, 512, 512], P(None, 'sector', None, 'section'), may hold values from -100 to 150, as said below
Outputs:
- probabilities: bfloat16 [98304, 8], P(('sector', 'section'))
- final_vectors: bfloat16 [98304, 512], P(('sector', 'section'))
Inputs may be any that keep to these rules, and one draw needn't show every extreme that they name: `sectors`: in the rows of one device no sector appears more than 36 times over all orbitals together, and on some device some sector appears exactly 36 times. Every block environments[k, q, s] is symmetric and positive definite.
All inputs are finite; a program needn't handle non-finite values.
Results may differ from a plain program's by a relative error of at most 0.0049.
Values may be sent and summed in bfloat16 or wider, within the bound.
No kernel may reach another device: no remote copies, remote signals or barrier semaphores. Data moves between devices by JAX's collectives and lax.ppermute only.
A program may use at most 128 MiB of HBM per device.

v0:
```python
import jax
import jax.numpy as jnp
from jax import lax
from jax.sharding import PartitionSpec as P

OUTCOMES = 4
ORBITALS = 2


def slot_positions(labels, sector_total):
    onehot = (labels[:, None] == jnp.arange(sector_total, dtype=jnp.int32)[None, :]).astype(
        jnp.int32
    )
    before = jnp.cumsum(onehot, axis=0) - onehot
    return jnp.sum(before * onehot, axis=1)


def branch_results(amplitudes, images, id_grid, block_width):
    weights = jnp.sum(images * amplitudes, axis=-1)
    norm_sum = jnp.sum(weights, axis=-1)
    filled = id_grid >= 0.0
    branch_probs = (weights / jnp.where(filled, norm_sum, 1.0)[..., None]).astype(jnp.bfloat16)
    chosen_mask = (id_grid[..., None] == jnp.arange(OUTCOMES, dtype=jnp.float32)).astype(
        jnp.float32
    )
    chosen_weight = jnp.sum(chosen_mask * weights, axis=-1)
    picked = jnp.sum(chosen_mask[..., None] * amplitudes, axis=-2)
    rescale = lax.rsqrt(jnp.where(filled, chosen_weight, 1.0) / block_width)
    advanced = (picked * rescale[..., None]).astype(jnp.bfloat16)
    return (branch_probs, advanced)


def local(vectors, sectors, outcomes, sites, environments):
    sector_count = lax.axis_size("sector")
    per_device = sites.shape[1]
    sector_total = per_device * sector_count
    sample_count = vectors.shape[0]
    block_width = vectors.shape[1]
    capacity = max(2, (3 * sample_count + sector_total - 1) // sector_total)
    current = vectors
    columns = []
    for orbital in range(ORBITALS):
        environ_k = lax.all_gather(environments[orbital], "section", axis=2, tiled=True)
        site_k = sites[orbital]
        labels = sectors[:, orbital]
        slot_of = labels * capacity + slot_positions(labels, sector_total)
        send_rows = (
            jnp.zeros((sector_total * capacity, block_width), jnp.bfloat16).at[slot_of].set(current)
        )
        send_rows = send_rows.reshape(sector_total, capacity, block_width)
        send_ids = (
            jnp.full((sector_total * capacity,), -1.0, jnp.bfloat16)
            .at[slot_of]
            .set(outcomes[:, orbital].astype(jnp.bfloat16))
        )
        send_ids = send_ids.reshape(sector_total, capacity)
        rows_in = lax.all_to_all(send_rows, "sector", split_axis=0, concat_axis=0, tiled=True)
        ids_in = lax.all_to_all(send_ids, "sector", split_axis=0, concat_axis=0, tiled=True)
        slot_count = rows_in.shape[1]
        arranged = rows_in.reshape(sector_count, per_device, slot_count, block_width)
        amplitudes = jnp.einsum(
            "iqcb,qbf->iqcf", arranged, site_k, preferred_element_type=jnp.float32
        )
        amplitudes = amplitudes.reshape(sector_count, per_device, slot_count, OUTCOMES, block_width)
        rounded = amplitudes.astype(jnp.bfloat16)
        images = jnp.einsum(
            "iqcsb,qsbe->iqcse", rounded, environ_k, preferred_element_type=jnp.float32
        )
        id_grid = ids_in.astype(jnp.float32).reshape(sector_count, per_device, slot_count)
        branch_probs, advanced = branch_results(amplitudes, images, id_grid, block_width)
        probs_back, rows_back = (
            lax.all_to_all(
                branch_probs.reshape(sector_total, slot_count, OUTCOMES),
                "sector",
                split_axis=0,
                concat_axis=0,
                tiled=True,
            ),
            lax.all_to_all(
                advanced.reshape(sector_total, slot_count, block_width),
                "sector",
                split_axis=0,
                concat_axis=0,
                tiled=True,
            ),
        )
        columns.append(probs_back.reshape(sector_total * capacity, OUTCOMES)[slot_of])
        current = rows_back.reshape(sector_total * capacity, block_width)[slot_of]
    return (jnp.concatenate(columns, axis=1), current)


def solution(mesh):
    placed = (
        P(("sector", "section"), None),
        P(("sector", "section"), None),
        P(("sector", "section"), None),
        P(None, "sector", None, None),
        P(None, "sector", None, "section", None),
    )
    return jax.shard_map(
        local,
        mesh=mesh,
        in_specs=placed,
        out_specs=(P(("sector", "section"), None), P(("sector", "section"), None)),
        check_vma=False,
    )
```

profile of v0, /device:TPU:1, one launch (start us, length us, event | category | flops | bytes accessed | tf_op | source)
XLA Modules:
  0.0 290.2 jit_solution(226082622245741807)
XLA Ops:
  17.0 6.4 %all-to-all-start.1 = ((bf16[8,4,36]{2,1,0:T(4,128)(2,1)}), bf16[8,4,36]{2,1,0:T(4,128)(2,1)S(1)}, u32[]{:S(2)}, u32[]{:S(2)}) async-start(bf16[8,4,36]{2,1,0:T(4,128)(2,1)} %all_to_all.31), calls=%async_computation.1 | async-start | bytes 16384 | tf_op jit(solution)/shard_map/all_to_all | solution.py:58
  28.0 4.8 %all-to-all-start = ((bf16[32,36,512]{2,1,0:T(8,128)(2,1)}), bf16[32,36,512]{2,1,0:T(8,128)(2,1)S(1)}, u32[]{:S(2)}, u32[]{:S(2)}) async-start(bf16[32,36,512]{2,1,0:T(8,128)(2,1)} %reshape.115), calls=%async_computation | async-start | bytes 2621440 | tf_op jit(solution)/shard_map/all_to_all | solution.py:57
  33.2 17.5 %all-to-all-done = bf16[32,36,512]{2,1,0:T(8,128)(2,1)S(1)} async-done(((bf16[32,36,512]{2,1,0:T(8,128)(2,1)}), bf16[32,36,512]{2,1,0:T(8,128)(2,1)S(1)}, u32[]{:S(2)}, u32[]{:S(2)}) %all-to-all-start) | async-done | bytes 1179680 | tf_op jit(solution)/shard_map/all_to_all | solution.py:57
  50.7 10.3 %fusion.12 = f32[8,4,36,2048]{3,2,0,1:T(8,128)} fusion(bf16[2,4,512,2048]{3,2,1,0:T(8,128)(2,1)} %param.8, bf16[8,4,36,512]{3,2,1,0:T(8,128)(2,1)S(1)} %bitcast.119), kind=kOutput, calls=%fused_computation.26 | convolution fusion | flops 2415919104 | bytes 19005440 | tf_op jit(solution)/shard_map/iqcb,qbf->iqcf/dot_general | solution.py:61
  60.9 12.0 %reshape.196 = f32[8,4,36,4,512]{4,3,2,0,1:T(4,128)} reshape(f32[8,4,36,2048]{3,2,0,1:T(8,128)} %fusion.12) | data formatting | bytes 18874368 | tf_op jit(solution)/shard_map/reshape | solution.py:64
  73.0 8.0 %multiply_reduce_fusion.1 = f32[8,4,36,512]{3,0,2,1:T(8,128)S(1)} fusion(f32[8,4,36,4,512]{4,3,2,0,1:T(4,128)} %reshape.196, f32[8,4,36,4]{3,0,2,1:T(8,128)S(1)} %copy.116), kind=kLoop, calls=%fused_computation.11 | loop fusion | flops 4128768 | bytes 11814912 | tf_op jit(solution)/shard_map/reduce_sum | solution.py:27
  81.0 3.5 %copy.117 = f32[8,4,36,512]{3,1,0,2:T(4,128)} copy(f32[8,4,36,512]{3,0,2,1:T(8,128)S(1)} %multiply_reduce_fusion.1) | data formatting | bytes 4718592 | tf_op jit(solution)/shard_map/reduce_sum | solution.py:27
  87.2 25.2 %all-gather.5.cloned.1.call-done = bf16[1,4,4,512,512]{4,3,2,1,0:T(8,128)(2,1)} async-done(((bf16[1,4,4,16,512]{4,3,2,1,0:T(8,128)(2,1)}), bf16[1,4,4,512,512]{4,3,2,1,0:T(8,128)(2,1)}) %all-gather.5.cloned.1.call-update) | async-done | bytes 8388624 | tf_op jit(solution)/shard_map/all_gather | solution.py:43
  112.3 19.2 %fusion.18 = (f32[8,4,36]{2,0,1:T(8,128)S(1)}, f32[8,4,36,4]{2,0,3,1:T(8,128)S(1)}) fusion(f32[8,4,36,4,512]{4,3,2,0,1:T(4,128)} %reshape.196, bf16[1,4,4,512,512]{4,3,2,1,0:T(8,128)(2,1)} %all-gather.5.cloned.1.call-done), kind=kOutput, calls=%fused_computation.28 | convolution fusion | flops 2422991360 | bytes 17848832 | tf_op jit(solution)/shard_map/iqcsb,qsbe->iqcse/dot_general | solution.py:66
  133.7 5.3 %all-to-all-start.3 = ((bf16[32,36,512]{2,1,0:T(8,128)(2,1)}), bf16[32,36,512]{2,1,0:T(8,128)(2,1)S(1)}, u32[]{:S(2)}, u32[]{:S(2)}) async-start(bf16[32,36,512]{2,1,0:T(8,128)(2,1)} %copy.122), calls=%async_computation.3 | async-start | bytes 2621440 | tf_op jit(solution)/shard_map/all_to_all | solution.py:79
  144.0 12.9 %all-to-all-done.3 = bf16[32,36,512]{2,1,0:T(8,128)(2,1)S(1)} async-done(((bf16[32,36,512]{2,1,0:T(8,128)(2,1)}), bf16[32,36,512]{2,1,0:T(8,128)(2,1)S(1)}, u32[]{:S(2)}, u32[]{:S(2)}) %all-to-all-start.3) | async-done | bytes 1179680 | tf_op jit(solution)/shard_map/all_to_all | solution.py:79
  156.9 4.1 %all-to-all-start.5 = ((bf16[8,4,36]{2,1,0:T(4,128)(2,1)}), bf16[8,4,36]{2,1,0:T(4,128)(2,1)S(1)}, u32[]{:S(2)}, u32[]{:S(2)}) async-start(bf16[8,4,36]{2,1,0:T(4,128)(2,1)} %all_to_all.36), calls=%async_computation.5 | async-start | bytes 16384 | tf_op jit(solution)/shard_map/all_to_all | solution.py:58
  161.3 4.1 %scatter_custom_fusion.2 = bf16[1152,512]{1,0:T(8,128)(2,1)S(1)} fusion(s32[384]{0:T(512)S(1)} %fusion.44, bf16[]{:T(256)} %constant.9.clone.1, bf16[1152,512]{1,0:T(8,128)(2,1)S(1)} %reshape.120, s32[1024]{0:T(1024)S(1)} %pad_clamp_fusion.1), kind=kCustom, calls=%fused_computation.36 | custom fusion | bytes 1179650 | tf_op jit(solution)/shard_map/scatter | solution.py:48
  166.6 4.8 %all-to-all-start.4 = ((bf16[32,36,512]{2,1,0:T(8,128)(2,1)}), bf16[32,36,512]{2,1,0:T(8,128)(2,1)S(1)}, u32[]{:S(2)}, u32[]{:S(2)}) async-start(bf16[32,36,512]{2,1,0:T(8,128)(2,1)} %reshape.121), calls=%async_computation.4 | async-start | bytes 2621440 | tf_op jit(solution)/shard_map/all_to_all | solution.py:57
  172.6 16.7 %all-to-all-done.4 = bf16[32,36,512]{2,1,0:T(8,128)(2,1)S(1)} async-done(((bf16[32,36,512]{2,1,0:T(8,128)(2,1)}), bf16[32,36,512]{2,1,0:T(8,128)(2,1)S(1)}, u32[]{:S(2)}, u32[]{:S(2)}) %all-to-all-start.4) | async-done | bytes 1179680 | tf_op jit(solution)/shard_map/all_to_all | solution.py:57
  189.3 4.3 %all-to-all-start.2 = ((bf16[8,2,288]{2,1,0:T(2,128)(2,1)}), bf16[8,2,288]{2,1,0:T(2,128)(2,1)S(1)}, u32[]{:S(2)}, u32[]{:S(2)}) async-start(bf16[8,2,288]{2,1,0:T(2,128)(2,1)} %reshape.222), calls=%async_computation.2 | async-start | bytes 24576 | tf_op jit(solution)/shard_map/all_to_all | solution.py:72
  193.6 10.3 %fusion.15 = f32[8,4,36,2048]{3,2,0,1:T(8,128)} fusion(bf16[2,4,512,2048]{3,2,1,0:T(8,128)(2,1)} %param.8, bf16[8,4,36,512]{3,2,1,0:T(8,128)(2,1)S(1)} %bitcast.118), kind=kOutput, calls=%fused_computation.27 | convolution fusion | flops 2415919104 | bytes 19005440 | tf_op jit(solution)/shard_map/iqcb,qbf->iqcf/dot_general | solution.py:61
  204.0 11.9 %reshape.197 = f32[8,4,36,4,512]{4,3,2,0,1:T(4,128)} reshape(f32[8,4,36,2048]{3,2,0,1:T(8,128)} %fusion.15) | data formatting | bytes 18874368 | tf_op jit(solution)/shard_map/reshape | solution.py:64
  215.9 19.1 %fusion.20 = (f32[8,4,36]{2,0,1:T(8,128)S(1)}, f32[8,4,36,4]{2,0,3,1:T(8,128)S(1)}) fusion(f32[8,4,36,4,512]{4,3,2,0,1:T(4,128)} %reshape.197, bf16[1,4,4,512,512]{4,3,2,1,0:T(8,128)(2,1)} %all-gather.7.cloned.1.call-done), kind=kOutput, calls=%fused_computation.30 | convolution fusion | flops 2422991360 | bytes 17848832 | tf_op jit(solution)/shard_map/iqcsb,qsbe->iqcse/dot_general | solution.py:66
  235.0 6.4 %multiply_reduce_fusion = f32[8,4,36,512]{3,0,2,1:T(8,128)S(1)} fusion(f32[8,4,36,4,512]{4,3,2,0,1:T(4,128)S(1)} %copy-done, f32[8,4,36,4]{3,0,2,1:T(8,128)S(1)} %copy.136), kind=kLoop, calls=%fused_computation.10 | loop fusion | flops 4128768 | bytes 11814912 | tf_op jit(solution)/shard_map/reduce_sum | solution.py:27
  241.6 3.5 %copy.137 = f32[8,4,36,512]{3,1,0,2:T(4,128)} copy(f32[8,4,36,512]{3,0,2,1:T(8,128)S(1)} %multiply_reduce_fusion) | data formatting | bytes 4718592 | tf_op jit(solution)/shard_map/reduce_sum | solution.py:27
  248.5 4.8 %all-to-all-start.6 = ((bf16[8,2,288]{2,1,0:T(2,128)(2,1)}), bf16[8,2,288]{2,1,0:T(2,128)(2,1)S(1)}, u32[]{:S(2)}, u32[]{:S(2)}) async-start(bf16[8,2,288]{2,1,0:T(2,128)(2,1)} %reshape.220), calls=%async_computation.6 | async-start | bytes 24576 | tf_op jit(solution)/shard_map/all_to_all | solution.py:72
  257.9 4.2 %all-to-all-start.7 = ((bf16[32,36,512]{2,1,0:T(8,128)(2,1)}), bf16[32,36,512]{2,1,0:T(8,128)(2,1)S(1)}, u32[]{:S(2)}, u32[]{:S(2)}) async-start(bf16[32,36,512]{2,1,0:T(8,128)(2,1)} %copy.142), calls=%async_computation.7 | async-start | bytes 2621440 | tf_op jit(solution)/shard_map/all_to_all | solution.py:79
  266.8 13.2 %all-to-all-done.7 = bf16[32,36,512]{2,1,0:T(8,128)(2,1)S(1)} async-done(((bf16[32,36,512]{2,1,0:T(8,128)(2,1)}), bf16[32,36,512]{2,1,0:T(8,128)(2,1)S(1)}, u32[]{:S(2)}, u32[]{:S(2)}) %all-to-all-start.7) | async-done | bytes 1179680 | tf_op jit(solution)/shard_map/all_to_all | solution.py:79
  (84 shorter events, 42.8 us)
Async XLA Ops:
  7.2 105.2 %all-gather.5.cloned.1.call-start = ((), (), s32[]{:S(2)}) async-start(), calls=%async_computation.8 | async-start | bytes 8650752 | tf_op jit(solution)/shard_map/all_gather | solution.py:43
  9.1 206.8 %all-gather.7.cloned.1.call-start = ((), (), s32[]{:S(2)}) async-start(), calls=%async_computation.9 | async-start | bytes 8650752 | tf_op jit(solution)/shard_map/all_gather | solution.py:43
  17.0 11.1 %all-to-all-start.1 = ((bf16[8,4,36]{2,1,0:T(4,128)(2,1)}), bf16[8,4,36]{2,1,0:T(4,128)(2,1)S(1)}, u32[]{:S(2)}, u32[]{:S(2)}) async-start(bf16[8,4,36]{2,1,0:T(4,128)(2,1)} %all_to_all.31), calls=%async_computation.1 | async-start | bytes 16384 | tf_op jit(solution)/shard_map/all_to_all | solution.py:58
  28.0 22.6 %all-to-all-start = ((bf16[32,36,512]{2,1,0:T(8,128)(2,1)}), bf16[32,36,512]{2,1,0:T(8,128)(2,1)S(1)}, u32[]{:S(2)}, u32[]{:S(2)}) async-start(bf16[32,36,512]{2,1,0:T(8,128)(2,1)} %reshape.115), calls=%async_computation | async-start | bytes 2621440 | tf_op jit(solution)/shard_map/all_to_all | solution.py:57
  131.9 8.3 %copy-start.1 = (s32[384,2]{0,1:T(2,128)S(1)}, s32[384,2]{0,1:T(2,128)}, u32[]{:S(2)}) copy-start(s32[384,2]{0,1:T(2,128)} %param.6) | copy-start | bytes 9220
  133.7 23.2 %all-to-all-start.3 = ((bf16[32,36,512]{2,1,0:T(8,128)(2,1)}), bf16[32,36,512]{2,1,0:T(8,128)(2,1)S(1)}, u32[]{:S(2)}, u32[]{:S(2)}) async-start(bf16[32,36,512]{2,1,0:T(8,128)(2,1)} %copy.122), calls=%async_computation.3 | async-start | bytes 2621440 | tf_op jit(solution)/shard_map/all_to_all | solution.py:79
  156.9 9.6 %all-to-all-start.5 = ((bf16[8,4,36]{2,1,0:T(4,128)(2,1)}), bf16[8,4,36]{2,1,0:T(4,128)(2,1)S(1)}, u32[]{:S(2)}, u32[]{:S(2)}) async-start(bf16[8,4,36]{2,1,0:T(4,128)(2,1)} %all_to_all.36), calls=%async_computation.5 | async-start | bytes 16384 | tf_op jit(solution)/shard_map/all_to_all | solution.py:58
  166.6 22.7 %all-to-all-start.4 = ((bf16[32,36,512]{2,1,0:T(8,128)(2,1)}), bf16[32,36,512]{2,1,0:T(8,128)(2,1)S(1)}, u32[]{:S(2)}, u32[]{:S(2)}) async-start(bf16[32,36,512]{2,1,0:T(8,128)(2,1)} %reshape.121), calls=%async_computation.4 | async-start | bytes 2621440 | tf_op jit(solution)/shard_map/all_to_all | solution.py:57
  189.3 59.2 %all-to-all-start.2 = ((bf16[8,2,288]{2,1,0:T(2,128)(2,1)}), bf16[8,2,288]{2,1,0:T(2,128)(2,1)S(1)}, u32[]{:S(2)}, u32[]{:S(2)}) async-start(bf16[8,2,288]{2,1,0:T(2,128)(2,1)} %reshape.222), calls=%async_computation.2 | async-start | bytes 24576 | tf_op jit(solution)/shard_map/all_to_all | solution.py:72
  215.9 19.2 %copy-start = (f32[8,4,36,4,512]{4,3,2,0,1:T(4,128)S(1)}, f32[8,4,36,4,512]{4,3,2,0,1:T(4,128)}, u32[]{:S(2)}) copy-start(f32[8,4,36,4,512]{4,3,2,0,1:T(4,128)} %reshape.197) | copy-start | bytes 28311556
  248.5 9.5 %all-to-all-start.6 = ((bf16[8,2,288]{2,1,0:T(2,128)(2,1)}), bf16[8,2,288]{2,1,0:T(2,128)(2,1)S(1)}, u32[]{:S(2)}, u32[]{:S(2)}) async-start(bf16[8,2,288]{2,1,0:T(2,128)(2,1)} %reshape.220), calls=%async_computation.6 | async-start | bytes 24576 | tf_op jit(solution)/shard_map/all_to_all | solution.py:72
  257.9 22.1 %all-to-all-start.7 = ((bf16[32,36,512]{2,1,0:T(8,128)(2,1)}), bf16[32,36,512]{2,1,0:T(8,128)(2,1)S(1)}, u32[]{:S(2)}, u32[]{:S(2)}) async-start(bf16[32,36,512]{2,1,0:T(8,128)(2,1)} %copy.142), calls=%async_computation.7 | async-start | bytes 2621440 | tf_op jit(solution)/shard_map/all_to_all | solution.py:79
Sparse Core Ops, SparseCore 0:
  10.6 101.7 all-gather.4
  115.5 95.3 all-gather.6
where the time goes:
time: 296 us; the launch traced here: 290 us
  waiting for transfers between devices  89.5 us (30%)
  local copies, waits for them, and re-layouts  68.9 us (23%)
  matrix products  58.9 us (20%)
  starting transfers between devices  38.9 us (13%)
  other arithmetic  19.1 us (6%)
  between operations  14.8 us (5%)
    dot_general x2, matrix products, local(): jnp.einsum('iqcsb,qsbe->iqcse', rounded, environ_k, preferred_element_typ...  38.3 us
    all_to_all x2, waiting for transfers between devices, local(): lax.all_to_all(send_rows, 'sector', split_axis=0, concat_axis=0, tiled=True)  34.2 us
    all_to_all x2, waiting for transfers between devices, local(): lax.all_to_all(advanced.reshape(sector_total, slot_count, block_width), '...  26.1 us
    all_gather x2, waiting for transfers between devices, local(): lax.all_gather(environments[orbital], 'section', axis=2, tiled=True)  25.2 us
    reshape x2, local copies, waits for them, and re-layouts, local(): amplitudes.reshape(sector_count, per_device, slot_count, OUTCOMES, block_...  23.9 us
    dot_general x2, matrix products, local(): jnp.einsum('iqcb,qbf->iqcf', arranged, site_k, preferred_element_type=jnp...  20.6 us
    reduce_sum x2, other arithmetic, branch_results(): picked = jnp.sum(chosen_mask[..., None] * amplitudes, axis=-2)  14.4 us
    reduce_sum x4, local copies, waits for them, and re-layouts, branch_results(): picked = jnp.sum(chosen_mask[..., None] * amplitudes, axis=-2)  12.3 us
  transfers between devices with their start and end apart: 10, of which 7 were waited for; matrix products, arithmetic and copies ran while one was open for 49% of the time, Pallas kernels for 0%

commit v1 on v0

v1 whole, which is shorter than its diff:
```python
import functools

import jax
import jax.numpy as jnp
from jax import lax
from jax.experimental import pallas as pl
from jax.experimental.pallas import tpu as pltpu
from jax.sharding import Mesh
from jax.sharding import PartitionSpec as P

OUTCOMES = 4
ORBITALS = 2
CAP = 36
MSG = 40
VMEM_LIMIT = 56 * 1024 * 1024

F32 = jnp.float32
BF16 = jnp.bfloat16


def vmem_specs(number):
    return [pl.BlockSpec(memory_space=pltpu.VMEM)] * number


def call(body, outs, *args, scratch=()):
    return pl.pallas_call(
        body,
        out_shape=outs,
        in_specs=vmem_specs(len(args)),
        out_specs=jax.tree.map(lambda _: pl.BlockSpec(memory_space=pltpu.VMEM), outs),
        scratch_shapes=list(scratch),
        compiler_params=pltpu.CompilerParams(vmem_limit_bytes=VMEM_LIMIT),
    )(*args)


def iota(shape, dim):
    return lax.broadcasted_iota(jnp.int32, shape, dim)


def mm(a, b):
    return jnp.dot(a, b, preferred_element_type=F32)


def as_bf16(mask):
    return jnp.where(mask, 1.0, 0.0).astype(BF16)


def column_ranks(labels):
    n = labels.shape[0]
    onehot = jnp.where(iota((n, 128), 1) == labels, 1.0, 0.0)
    earlier = as_bf16(iota((n, n), 1) < iota((n, n), 0))
    return jnp.sum(mm(earlier, onehot.astype(BF16)) * onehot, axis=1, keepdims=True).astype(
        jnp.int32
    )


def row_ranks(labels):
    n = labels.shape[1]
    onehot = jnp.where(iota((128, n), 0) == labels, 1.0, 0.0)
    earlier = as_bf16(iota((n, n), 0) < iota((n, n), 1))
    return jnp.sum(mm(onehot.astype(BF16), earlier) * onehot, axis=0, keepdims=True).astype(
        jnp.int32
    )


def filled_messages(rows, labels_row, ranks_row, ranks_col, codes_col, slots):
    n = rows.shape[0]
    place = as_bf16(iota((slots, n), 0) == labels_row * MSG + ranks_row)
    heads = as_bf16(iota((slots, n), 0) == labels_row * MSG + CAP)
    codes = jnp.where(iota((n, 128), 1) == ranks_col, codes_col, 0.0).astype(BF16)
    return mm(place, rows), mm(heads, codes)


def first_kernel(vec_ref, sec_ref, sect_ref, out_ref, send_ref, ranks_ref, ranks_row_ref):
    slots = send_ref.shape[0]
    sec, sect = sec_ref[...], sect_ref[...]
    cols = [column_ranks(sec[:, k : k + 1]) for k in range(ORBITALS)]
    rows = [row_ranks(sect[k : k + 1, :]) for k in range(ORBITALS)]
    codes = (out_ref[:, 0:1] + 1).astype(F32)
    data, heads = filled_messages(vec_ref[...], sect[0:1, :], rows[0], cols[0], codes, slots)
    send_ref[...] = data.astype(BF16)
    send_ref[:, 0:128] = (data[:, 0:128] + heads).astype(BF16)
    ranks_ref[...] = jnp.concatenate(cols, axis=1)
    ranks_row_ref[...] = jnp.concatenate(rows, axis=0)


def gathered_probs(back, labels_col, ranks_col, slots):
    n = labels_col.shape[0]
    lanes = back[:, 0:128]
    found = []
    for s in range(OUTCOMES):
        pick = as_bf16(iota((n, slots), 1) == labels_col * MSG + (CAP + s))
        line = mm(pick, lanes)
        found.append(
            jnp.sum(jnp.where(iota((n, 128), 1) == ranks_col, line, 0.0), axis=1, keepdims=True)
        )
    return found


def middle_kernel(back_ref, sec_ref, sect_ref, out_ref, ranks_ref, ranks_row_ref, send_ref):
    slots, n = back_ref.shape[0], sec_ref.shape[0]
    pick = as_bf16(iota((n, slots), 1) == sec_ref[:, 0:1] * MSG + ranks_ref[:, 0:1])
    current = mm(pick, back_ref[...]).astype(BF16)
    codes = (out_ref[:, 1:2] + 1).astype(F32)
    data, heads = filled_messages(
        current, sect_ref[1:2, :], ranks_row_ref[1:2, :], ranks_ref[:, 1:2], codes, slots
    )
    send_ref[...] = data.astype(BF16)
    send_ref[:, 0:128] = (data[:, 0:128] + heads).astype(BF16)


def probs_kernel(back_ref, sec_ref, ranks_ref, probs_ref):
    found = gathered_probs(back_ref[...], sec_ref[:, 0:1], ranks_ref[:, 0:1], back_ref.shape[0])
    probs_ref[...] = jnp.concatenate(found, axis=1).astype(BF16)


def last_kernel(back_ref, sec_ref, ranks_ref, probs0_ref, probs_ref, final_ref):
    slots, n = back_ref.shape[0], sec_ref.shape[0]
    back = back_ref[...]
    pick = as_bf16(iota((n, slots), 1) == sec_ref[:, 1:2] * MSG + ranks_ref[:, 1:2])
    final_ref[...] = mm(pick, back).astype(BF16)
    found = gathered_probs(back, sec_ref[:, 1:2], ranks_ref[:, 1:2], slots)
    probs_ref[:, 0:OUTCOMES] = probs0_ref[...]
    probs_ref[:, OUTCOMES : 2 * OUTCOMES] = jnp.concatenate(found, axis=1).astype(BF16)


def pack_kernel(at_ref, env_ref, packed_ref):
    twice = jnp.where(pl.program_id(0) == 1, 2.0, 1.0)
    packed_ref[...] = jnp.swapaxes(env_ref[...].astype(F32) * twice, 0, 1).astype(BF16)


def packed_environments(env, at):
    ks, qs, ss, rs, cs = env.shape
    tile = cs // 4
    return pl.pallas_call(
        pack_kernel,
        out_shape=jax.ShapeDtypeStruct((qs, ks, ss, rs, 3 * tile), BF16),
        grid_spec=pltpu.PrefetchScalarGridSpec(
            num_scalar_prefetch=1,
            grid=(3,),
            in_specs=[
                pl.BlockSpec(
                    (ks, qs, ss, rs, tile), lambda t, at: (0, 0, 0, 0, lax.rem(at[0] + t, 4))
                )
            ],
            out_specs=pl.BlockSpec((qs, ks, ss, rs, tile), lambda t, at: (0, 0, 0, 0, t)),
        ),
    )(at, env)


def stage_kernel(rows_ref, site_ref, packed_ref, back_ref, env_ref, picked_ref):
    width = rows_ref.shape[1]
    tile = width // 4
    chunk = 8 * MSG
    per = packed_ref.shape[0] // 4
    zero = jnp.zeros((tile, tile), BF16)
    for s in range(OUTCOMES):
        for i in range(4):
            own = packed_ref[per * i : per * (i + 1), s].reshape(tile, 3 * tile)
            for t in range(3):
                j = (i + t) % 4
                env_ref[s, tile * i : tile * (i + 1), tile * j : tile * (j + 1)] = own[
                    :, tile * t : tile * (t + 1)
                ]
            j = (i + 3) % 4
            env_ref[s, tile * i : tile * (i + 1), tile * j : tile * (j + 1)] = zero

    def message_of(index):
        return jnp.floor((index.astype(F32) + 0.5) * (1.0 / MSG)).astype(jnp.int32)

    square = (chunk, chunk)
    across, down = iota(square, 1), iota(square, 0)
    head = message_of(down) * MSG + CAP
    spread = as_bf16(across == head)
    sub = iota((chunk, 128), 0)
    within = sub - message_of(sub) * MSG
    diagonal = iota((chunk, 128), 1) == within
    head_t = message_of(across) * MSG + CAP
    rises = [as_bf16(down == head_t + s) for s in range(OUTCOMES)]
    in_data = within[:, 0:1] < CAP

    def step(number, carry):
        at = pl.ds(pl.multiple_of(number * chunk, chunk), chunk)
        rows = rows_ref[at, :]
        code = jnp.sum(
            jnp.where(diagonal, mm(spread, rows[:, 0:128]), 0.0), axis=1, keepdims=True
        )
        code = jnp.where(in_data, code, 0.0)
        weights = []
        for s in range(OUTCOMES):
            amplitudes = mm(rows, site_ref[:, width * s : width * (s + 1)])
            images = mm(amplitudes.astype(BF16), env_ref[s])
            weights.append(jnp.sum(images * amplitudes, axis=1, keepdims=True))
            chosen = code == (s + 1.0)
            if s == 0:
                picked_ref[...] = jnp.where(chosen, amplitudes, 0.0)
            else:
                picked_ref[...] = jnp.where(chosen, amplitudes, picked_ref[...])
        filled = code > 0.0
        total = jnp.where(filled, weights[0] + weights[1] + weights[2] + weights[3], 1.0)
        lines = jnp.zeros((chunk, 128), F32)
        chosen_weight = jnp.zeros((chunk, 1), F32)
        for s in range(OUTCOMES):
            prob = jnp.where(filled, weights[s] / total, 0.0)
            lines += mm(rises[s], jnp.where(diagonal, prob, 0.0).astype(BF16))
            chosen_weight = jnp.where(code == (s + 1.0), weights[s], chosen_weight)
        scale = lax.rsqrt(jnp.where(filled, chosen_weight, 1.0) / width)
        picked = picked_ref[...] * scale
        back_ref[at, :] = picked.astype(BF16)
        back_ref[at, 0:128] = (picked[:, 0:128] + lines).astype(BF16)
        return carry

    lax.fori_loop(0, rows_ref.shape[0] // chunk, step, 0)


def local(vectors, sectors, outcomes, sites, environments, holders):
    n, width = vectors.shape
    sector_total = sites.shape[1] * lax.axis_size("sector")
    slots = sector_total * MSG
    mine = lax.axis_index("part")
    shape = functools.partial(jax.ShapeDtypeStruct)

    at = (lax.axis_index("row") * 4 // lax.axis_size("row")).astype(jnp.int32).reshape(1)
    packed = packed_environments(environments, at)
    packed = lax.all_to_all(packed, "part", split_axis=0, concat_axis=0, tiled=True)
    envs = [
        lax.all_gather(packed[:, k], "row", axis=0, tiled=True) for k in range(ORBITALS)
    ]

    flipped = sectors.T
    send, ranks, ranks_row = call(
        first_kernel,
        (
            shape((slots, width), BF16),
            shape((n, ORBITALS), jnp.int32),
            shape((ORBITALS, n), jnp.int32),
        ),
        vectors,
        sectors,
        flipped,
        outcomes,
    )

    def exchanged(messages):
        messages = messages.reshape(sector_total, MSG, width)
        messages = lax.all_to_all(messages, holders, split_axis=0, concat_axis=0, tiled=True)
        return messages.reshape(slots, width)

    def stage(k, messages):
        site = lax.dynamic_index_in_dim(sites[k], mine, 0, keepdims=False)
        return call(
            stage_kernel,
            shape((slots, width), BF16),
            messages,
            site,
            envs[k],
            scratch=(
                pltpu.VMEM((OUTCOMES, width, width), BF16),
                pltpu.VMEM((8 * MSG, width), F32),
            ),
        )

    back = exchanged(stage(0, exchanged(send)))
    send = call(
        middle_kernel, shape((slots, width), BF16), back, sectors, flipped, outcomes, ranks, ranks_row
    )
    probs0 = call(probs_kernel, shape((n, OUTCOMES), BF16), back, sectors, ranks)
    back = exchanged(stage(1, exchanged(send)))
    return call(
        last_kernel,
        (shape((n, ORBITALS * OUTCOMES), BF16), shape((n, width), BF16)),
        back,
        sectors,
        ranks,
        probs0,
    )


def solution(mesh):
    sector, section = mesh.devices.shape

    def whole(vectors, sectors, outcomes, sites, environments):
        parts = sites.shape[1] // sector
        fine = Mesh(
            mesh.devices.reshape(sector, section // parts, parts), ("sector", "row", "part")
        )
        split = P(("sector", "row", "part"), None)
        return jax.shard_map(
            functools.partial(local, holders=("sector", "part")),
            mesh=fine,
            in_specs=(
                split,
                split,
                split,
                P(None, "sector", None, None),
                P(None, "sector", None, ("row", "part"), None),
            ),
            out_specs=(split, split),
            check_vma=False,
        )(vectors, sectors, outcomes, sites, environments)

    return whole
```

time: 296 us -> 187 us (0.63); the launches traced: 290 us -> 186 us
  matrix products: 58.9 us -> 0 us
  waiting for transfers between devices: 89.5 us -> 42.2 us
  Pallas kernels: 0 us -> 45.6 us
  local copies, waits for them, and re-layouts: 68.9 us -> 24.6 us
  blocking collectives: 0 us -> 42.9 us
  starting transfers between devices: 38.9 us -> 17 us
  other arithmetic: 19.1 us -> 0 us
    dot_general x4 -> x0, matrix products: 58.9 us -> none  [the longest x2 38.3 us: local(): jnp.einsum('iqcsb,qsbe->iqcse', rounded, environ_k, preferred_element_typ...]
    pallas_call x0 -> x7, Pallas kernels: none -> 45.6 us  [the longest x6 43 us: call(): pl.pallas_call(body, out_shape=outs, in_specs=vmem_specs(len(args)), out_...]
    all_to_all x0 -> x2, blocking collectives: none -> 42.9 us  [the longest x1 31.6 us: exchanged(): lax.all_to_all(messages, holders, split_axis=0, concat_axis=0, tiled=True)]
    all_to_all x8 -> x3, waiting for transfers between devices: 63.6 us -> 35 us  [exchanged(): lax.all_to_all(messages, holders, split_axis=0, concat_axis=0, tiled=True)]
    reshape x10 -> x0, local copies, waits for them, and re-layouts: 27.6 us -> none  [the longest x2 23.9 us: local(): amplitudes.reshape(sector_count, per_device, slot_count, OUTCOMES, block_...]
    all_to_all x8 -> x3, starting transfers between devices: 38.8 us -> 17 us  [exchanged(): lax.all_to_all(messages, holders, split_axis=0, concat_axis=0, tiled=True)]
    all_gather x2, waiting for transfers between devices: 25.2 us -> 7.11 us  [local(): lax.all_gather(packed[:, k], 'row', axis=0, tiled=True)]
    reduce_sum x6 -> x0, other arithmetic: 14.6 us -> none  [the longest x2 14.4 us: branch_results(): picked = jnp.sum(chosen_mask[..., None] * amplitudes, axis=-2)]
  transfers between devices with their start and end apart: 10 -> 5, of which waited for: 7 -> 4; matrix products, arithmetic and copies ran while one was open for 49% -> 11% of each run, Pallas kernels for 0% -> 14%
where the time goes in v1:
time: 187 us; the launch traced here: 186 us
  Pallas kernels  45.6 us (24%)
  blocking collectives  42.9 us (23%)
  waiting for transfers between devices  42.2 us (23%)
  local copies, waits for them, and re-layouts  24.6 us (13%)
  starting transfers between devices  17 us (9%)
  between operations  14.1 us (8%)
    pallas_call x6, Pallas kernels, call(): pl.pallas_call(body, out_shape=outs, in_specs=vmem_specs(len(args)), out_...  43 us
    all_to_all x3, waiting for transfers between devices, exchanged(): lax.all_to_all(messages, holders, split_axis=0, concat_axis=0, tiled=True)  35 us
    all_to_all x1, blocking collectives, exchanged(): lax.all_to_all(messages, holders, split_axis=0, concat_axis=0, tiled=True)  31.6 us
    all_to_all x3, starting transfers between devices, exchanged(): lax.all_to_all(messages, holders, split_axis=0, concat_axis=0, tiled=True)  17 us
    slice x1, local copies, waits for them, and re-layouts, stage(): site = lax.dynamic_index_in_dim(sites[k], mine, 0, keepdims=False)  11.9 us
    all_to_all x1, blocking collectives, local(): lax.all_to_all(packed, 'part', split_axis=0, concat_axis=0, tiled=True)  11.3 us
    all_gather x2, waiting for transfers between devices, local(): lax.all_gather(packed[:, k], 'row', axis=0, tiled=True)  7.11 us
    squeeze x2, local copies, waits for them, and re-layouts, stage(): site = lax.dynamic_index_in_dim(sites[k], mine, 0, keepdims=False)  6.43 us
  transfers between devices with their start and end apart: 5, of which 4 were waited for; matrix products, arithmetic and copies ran while one was open for 11% of the time, Pallas kernels for 14%

profile of v1, /device:TPU:1, one launch (start us, length us, event | category | flops | bytes accessed | tf_op | source)
XLA Modules:
  0.0 186.4 jit_solution(10426527955939857213)
XLA Ops:
  7.2 2.6 %shard_map.69 = bf16[4,2,4,16,384]{4,3,2,1,0:T(8,128)(2,1)} custom-call(s32[1]{0:T(128)} %bitcast.4.at_ref, bf16[2,4,4,16,512]{4,3,2,1,0:T(8,128)(2,1)} %env_ref.1), custom_call_target="tpu_custom_call" | custom-call | tf_op jit(solution)/shard_map/pallas_call | solution.py:135
  9.9 11.3 %all_to_all.25 = bf16[4,2,4,16,384]{4,3,2,1,0:T(8,128)(2,1)S(1)} all-to-all(bf16[4,2,4,16,384]{4,3,2,1,0:T(8,128)(2,1)} %shard_map.69), channel_id=1, replica_groups=mesh['sector'=8,'row'=8,'part'=4] {'part'}, dimensions={0} | all-to-all | bytes 786432 | tf_op jit(solution)/shard_map/all_to_all | solution.py:225
  22.0 0.9 copy.15.sec_ref
  22.9 0.8 copy.16.out_ref
  23.7 3.9 %shard_map.68 = (bf16[1280,512]{1,0:T(8,128)(2,1)}, s32[384,2]{1,0:T(8,128)}, s32[2,384]{1,0:T(2,128)}) custom-call(bf16[384,512]{1,0:T(8,128)(2,1)} %vec_ref.1, s32[384,2]{1,0:T(8,128)} %copy.15.sec_ref, s32[2,384]{1,0:T(2,128)} %bitcast.27, s32[384,2]{1,0:T(8,128)} %copy.16.out_ref), custom_call_target="tpu_custom_call" | custom-call | tf_op jit(solution)/shard_map/pallas_call | solution.py:26
  27.6 7.8 %all-to-all-start = ((bf16[32,40,512]{2,1,0:T(8,128)(2,1)}), bf16[32,40,512]{2,1,0:T(8,128)(2,1)S(1)}, u32[]{:S(2)}, u32[]{:S(2)}) async-start(bf16[32,40,512]{2,1,0:T(8,128)(2,1)} %bitcast.26), calls=%async_computation | async-start | bytes 2621440 | tf_op jit(solution)/shard_map/all_to_all | solution.py:246
  35.5 11.9 %fusion = (bf16[1,4,512,2048]{3,2,1,0:T(8,128)(2,1)}, bf16[1,4,512,2048]{3,2,1,0:T(8,128)(2,1)}) fusion(bf16[2,4,512,2048]{3,2,1,0:T(8,128)(2,1)} %param.8), kind=kLoop, calls=%fused_computation.2 | loop fusion | bytes 33554432 | tf_op jit(solution)/shard_map/slice | solution.py:250
  47.4 3.2 %dynamic-slice_bitcast_fusion.1.site_ref = bf16[512,2048]{1,0:T(8,128)(2,1)} fusion(bf16[1,4,512,2048]{3,2,1,0:T(8,128)(2,1)} %get-tuple-element.13, s32[]{:T(128)S(6)} %select_n.10), kind=kLoop, calls=%fused_computation.1 | loop fusion | bytes 4194308 | tf_op jit(solution)/shard_map/jit(dynamic_index_in_dim)/squeeze | solution.py:250
  50.6 3.7 %all-to-all-done = bf16[32,40,512]{2,1,0:T(8,128)(2,1)S(1)} async-done(((bf16[32,40,512]{2,1,0:T(8,128)(2,1)}), bf16[32,40,512]{2,1,0:T(8,128)(2,1)S(1)}, u32[]{:S(2)}, u32[]{:S(2)}) %all-to-all-start) | async-done | bytes 1310752 | tf_op jit(solution)/shard_map/all_to_all | solution.py:246
  54.3 7.1 %all-gather.5.cloned.1.call-done = bf16[32,1,4,16,384]{4,3,2,1,0:T(8,128)(2,1)} async-done(((bf16[4,1,4,16,384]{4,3,2,1,0:T(8,128)(2,1)}), bf16[32,1,4,16,384]{4,3,2,1,0:T(8,128)(2,1)}) %all-gather.5.cloned.1.call-update) | async-done | bytes 1572880 | tf_op jit(solution)/shard_map/all_gather | solution.py:227
  61.4 13.6 %shard_map.70 = bf16[1280,512]{1,0:T(8,128)(2,1)} custom-call(bf16[1280,512]{1,0:T(8,128)(2,1)} %bitcast.20, bf16[512,2048]{1,0:T(8,128)(2,1)} %dynamic-slice_bitcast_fusion.1.site_ref, bf16[32,4,16,384]{3,2,1,0:T(8,128)(2,1)} %bitcast.24), custom_call_target="tpu_custom_call" | custom-call | tf_op jit(solution)/shard_map/pallas_call | solution.py:26
  75.0 31.6 %all_to_all.26 = bf16[32,40,512]{2,1,0:T(8,128)(2,1)} all-to-all(bf16[32,40,512]{2,1,0:T(8,128)(2,1)} %bitcast.23), channel_id=1, replica_groups=mesh['sector'=8,'row'=8,'part'=4] {'sector','part'}, dimensions={0} | all-to-all | bytes 2621440 | tf_op jit(solution)/shard_map/all_to_all | solution.py:246
  106.6 4.4 %shard_map.71 = bf16[1280,512]{1,0:T(8,128)(2,1)} custom-call(bf16[1280,512]{1,0:T(8,128)(2,1)} %bitcast.16, s32[384,2]{1,0:T(8,128)} %copy.15.sec_ref, s32[2,384]{1,0:T(2,128)} %bitcast.28, s32[384,2]{1,0:T(8,128)} %copy.16.out_ref, s32[384,2]{1,0:T(8,128)} %get-tuple-element.6.ranks_ref, s32[2,384]{1,0:T(2,128)} %get-tuple-element.7.ranks_row_ref), custom_call_target="tpu_custom_call" | custom-call | tf_op jit(solution)/shard_map/pallas_call | solution.py:26
  111.0 4.2 %all-to-all-start.3 = ((bf16[32,40,512]{2,1,0:T(8,128)(2,1)}), bf16[32,40,512]{2,1,0:T(8,128)(2,1)S(1)}, u32[]{:S(2)}, u32[]{:S(2)}) async-start(bf16[32,40,512]{2,1,0:T(8,128)(2,1)} %bitcast.19), calls=%async_computation.3 | async-start | bytes 2621440 | tf_op jit(solution)/shard_map/all_to_all | solution.py:246
  115.3 3.2 %dynamic-slice_bitcast_fusion.site_ref = bf16[512,2048]{1,0:T(8,128)(2,1)} fusion(bf16[1,4,512,2048]{3,2,1,0:T(8,128)(2,1)} %get-tuple-element.12, s32[]{:T(128)S(6)} %select_n.10), kind=kLoop, calls=%fused_computation | loop fusion | bytes 4194308 | tf_op jit(solution)/shard_map/jit(dynamic_index_in_dim)/squeeze | solution.py:250
  118.5 15.7 %all-to-all-done.3 = bf16[32,40,512]{2,1,0:T(8,128)(2,1)S(1)} async-done(((bf16[32,40,512]{2,1,0:T(8,128)(2,1)}), bf16[32,40,512]{2,1,0:T(8,128)(2,1)S(1)}, u32[]{:S(2)}, u32[]{:S(2)}) %all-to-all-start.3) | async-done | bytes 1310752 | tf_op jit(solution)/shard_map/all_to_all | solution.py:246
  134.3 1.1 copy-done.2
  135.3 13.6 %shard_map.72 = bf16[1280,512]{1,0:T(8,128)(2,1)} custom-call(bf16[1280,512]{1,0:T(8,128)(2,1)} %bitcast.21, bf16[512,2048]{1,0:T(8,128)(2,1)} %dynamic-slice_bitcast_fusion.site_ref, bf16[32,4,16,384]{3,2,1,0:T(8,128)(2,1)} %bitcast.25), custom_call_target="tpu_custom_call" | custom-call | tf_op jit(solution)/shard_map/pallas_call | solution.py:26
  148.9 4.9 %all-to-all-start.4 = ((bf16[32,40,512]{2,1,0:T(8,128)(2,1)}), bf16[32,40,512]{2,1,0:T(8,128)(2,1)S(1)}, u32[]{:S(2)}, u32[]{:S(2)}) async-start(bf16[32,40,512]{2,1,0:T(8,128)(2,1)} %bitcast.22), calls=%async_computation.4 | async-start | bytes 2621440 | tf_op jit(solution)/shard_map/all_to_all | solution.py:246
  153.8 3.4 %shard_map.73.probs0_ref = bf16[384,4]{1,0:T(8,128)(2,1)} custom-call(bf16[1280,512]{1,0:T(8,128)(2,1)} %bitcast.17, s32[384,2]{1,0:T(8,128)} %copy.15.sec_ref, s32[384,2]{1,0:T(8,128)} %get-tuple-element.6.ranks_ref), custom_call_target="tpu_custom_call" | custom-call | tf_op jit(solution)/shard_map/pallas_call | solution.py:26
  157.2 15.6 %all-to-all-done.4 = bf16[32,40,512]{2,1,0:T(8,128)(2,1)S(1)} async-done(((bf16[32,40,512]{2,1,0:T(8,128)(2,1)}), bf16[32,40,512]{2,1,0:T(8,128)(2,1)S(1)}, u32[]{:S(2)}, u32[]{:S(2)}) %all-to-all-start.4) | async-done | bytes 1310752 | tf_op jit(solution)/shard_map/all_to_all | solution.py:246
  172.8 1.1 copy-done
  173.9 4.1 %shard_map.74 = (bf16[384,8]{1,0:T(8,128)(2,1)}, bf16[384,512]{1,0:T(8,128)(2,1)}) custom-call(bf16[1280,512]{1,0:T(8,128)(2,1)} %bitcast.18, s32[384,2]{1,0:T(8,128)} %copy.15.sec_ref, s32[384,2]{1,0:T(8,128)} %get-tuple-element.6.ranks_ref, bf16[384,4]{1,0:T(8,128)(2,1)} %shard_map.73.probs0_ref), custom_call_target="tpu_custom_call" | custom-call | tf_op jit(solution)/shard_map/pallas_call | solution.py:26
  178.0 1.6 copy.21
  (14 shorter events, 0.9 us)
Async XLA Ops:
  7.2 14.8 %copy-start.3 = (s32[384,2]{0,1:T(2,128)S(1)}, s32[384,2]{0,1:T(2,128)}, u32[]{:S(2)}) copy-start(s32[384,2]{0,1:T(2,128)} %param.6) | copy-start | bytes 9220
  7.2 15.7 %copy-start.4 = (s32[384,2]{0,1:T(2,128)S(1)}, s32[384,2]{0,1:T(2,128)}, u32[]{:S(2)}) copy-start(s32[384,2]{0,1:T(2,128)} %param.7) | copy-start | bytes 9220
  7.2 54.2 %all-gather.5.cloned.1.call-start = ((), (), s32[]{:S(2)}) async-start(), calls=%async_computation.5 | async-start | bytes 1769472 | tf_op jit(solution)/shard_map/all_gather | solution.py:227
  27.6 26.7 %all-to-all-start = ((bf16[32,40,512]{2,1,0:T(8,128)(2,1)}), bf16[32,40,512]{2,1,0:T(8,128)(2,1)S(1)}, u32[]{:S(2)}, u32[]{:S(2)}) async-start(bf16[32,40,512]{2,1,0:T(8,128)(2,1)} %bitcast.26), calls=%async_computation | async-start | bytes 2621440 | tf_op jit(solution)/shard_map/all_to_all | solution.py:246
  35.4 83.1 %all-gather.7.cloned.1.call-start = ((), (), s32[]{:S(2)}) async-start(), calls=%async_computation.6 | async-start | bytes 1769472 | tf_op jit(solution)/shard_map/all_gather | solution.py:227
  54.3 7.1 %copy-start.1 = (bf16[32,40,512]{2,1,0:T(8,128)(2,1)}, bf16[32,40,512]{2,1,0:T(8,128)(2,1)S(1)}, u32[]{:S(2)}) copy-start(bf16[32,40,512]{2,1,0:T(8,128)(2,1)S(1)} %all-to-all-done) | copy-start | bytes 3932164
  111.0 23.2 %all-to-all-start.3 = ((bf16[32,40,512]{2,1,0:T(8,128)(2,1)}), bf16[32,40,512]{2,1,0:T(8,128)(2,1)S(1)}, u32[]{:S(2)}, u32[]{:S(2)}) async-start(bf16[32,40,512]{2,1,0:T(8,128)(2,1)} %bitcast.19), calls=%async_computation.3 | async-start | bytes 2621440 | tf_op jit(solution)/shard_map/all_to_all | solution.py:246
  134.3 1.1 copy-start.2
  148.9 23.9 %all-to-all-start.4 = ((bf16[32,40,512]{2,1,0:T(8,128)(2,1)}), bf16[32,40,512]{2,1,0:T(8,128)(2,1)S(1)}, u32[]{:S(2)}, u32[]{:S(2)}) async-start(bf16[32,40,512]{2,1,0:T(8,128)(2,1)} %bitcast.22), calls=%async_computation.4 | async-start | bytes 2621440 | tf_op jit(solution)/shard_map/all_to_all | solution.py:246
  172.8 1.1 copy-start
Sparse Core Ops, SparseCore 0:
  22.1 39.2 all-gather.4
  63.2 38.6 all-gather.6

commit v2 on v0

v2 whole, which is shorter than its diff:
```python
import functools

import jax
import jax.numpy as jnp
from jax import lax
from jax.experimental import pallas as pl
from jax.experimental.pallas import tpu as pltpu
from jax.sharding import Mesh
from jax.sharding import PartitionSpec as P

OUTCOMES = 4
ORBITALS = 2
CAP = 36
MSG = 40
LANES = 128
VMEM_LIMIT = 56 * 1024 * 1024

F32 = jnp.float32
BF16 = jnp.bfloat16


def shape(dims, kind):
    return jax.ShapeDtypeStruct(dims, kind)


def near(x):
    return pltpu.with_memory_space_constraint(x, pltpu.VMEM)


def call(body, outs, *args):
    vmem = pl.BlockSpec(memory_space=pltpu.VMEM)
    return pl.pallas_call(
        body,
        out_shape=outs,
        in_specs=[vmem] * len(args),
        out_specs=jax.tree.map(lambda _: vmem, outs),
        compiler_params=pltpu.CompilerParams(vmem_limit_bytes=VMEM_LIMIT),
    )(*[near(x) for x in args])


def iota(dims, dim):
    return lax.broadcasted_iota(jnp.int32, dims, dim)


def mm(a, b):
    return jnp.dot(a, b, preferred_element_type=F32)


def as_bf16(mask, value=1.0):
    return jnp.where(mask, value, 0.0).astype(BF16)


SECTOR, RANK, CODE = 0, 2, 4


def index_table(sectors, outcomes):
    n = sectors.shape[1]
    earlier = as_bf16(iota((n, n), 0) < iota((n, n), 1))
    ranks = []
    for k in range(ORBITALS):
        onehot = jnp.where(iota((LANES, n), 0) == sectors[k : k + 1, :], 1.0, 0.0)
        before = mm(onehot.astype(BF16), earlier)
        ranks.append(jnp.sum(before * onehot, axis=0, keepdims=True))
    return jnp.concatenate(
        [
            sectors.astype(F32),
            *ranks,
            outcomes.astype(F32) + 1.0,
            jnp.zeros((8 - 3 * ORBITALS, n), F32),
        ],
        axis=0,
    )


def fill_messages(send_ref, rows, k, table, columns):
    slots, n = send_ref.shape[0], rows.shape[0]
    first = table[SECTOR + k : SECTOR + k + 1, :] * MSG
    slot = first + table[RANK + k : RANK + k + 1, :]
    at = iota((slots, n), 0)
    data = mm(as_bf16(at == slot.astype(jnp.int32)), rows)
    send_ref[...] = data.astype(BF16)
    codes = as_bf16(
        iota((n, LANES), 1) == columns[:, RANK + k : RANK + k + 1].astype(jnp.int32),
        columns[:, CODE + k : CODE + k + 1],
    )
    heads = as_bf16(iota((LANES, n), 0) == table[SECTOR + k : SECTOR + k + 1, :].astype(jnp.int32))
    lines = mm(heads, codes)[: slots // MSG]
    in_head = iota((slots // MSG, MSG, LANES), 1) == CAP
    front = data[:, :LANES].reshape(slots // MSG, MSG, LANES)
    front = jnp.where(in_head, lines[:, None, :], front)
    send_ref[:, :LANES] = front.reshape(slots, LANES).astype(BF16)


def picked_rows(back, k, columns):
    slots, n = back.shape[0], columns.shape[0]
    slot = columns[:, SECTOR + k : SECTOR + k + 1] * MSG + columns[:, RANK + k : RANK + k + 1]
    return mm(as_bf16(iota((n, slots), 1) == slot.astype(jnp.int32)), back).astype(BF16)


def picked_probs(back, k, columns):
    slots, n = back.shape[0], columns.shape[0]
    messages = slots // MSG
    front = back[:, :LANES].astype(F32).reshape(messages, MSG, LANES)
    of = as_bf16(
        iota((n, messages), 1) == columns[:, SECTOR + k : SECTOR + k + 1].astype(jnp.int32)
    )
    here = iota((n, LANES), 1) == columns[:, RANK + k : RANK + k + 1].astype(jnp.int32)
    found = []
    for s in range(OUTCOMES):
        lines = mm(of, front[:, CAP + s, :].astype(BF16))
        found.append(jnp.sum(jnp.where(here, lines, 0.0), axis=1, keepdims=True))
    return found


def first_kernel(vec_ref, sec_ref, out_ref, send_ref, table_ref, columns_ref):
    table = index_table(sec_ref[...], out_ref[...])
    columns = table.T
    table_ref[...] = table
    columns_ref[...] = columns
    fill_messages(send_ref, vec_ref[...], 0, table, columns)


def middle_kernel(back_ref, table_ref, columns_ref, send_ref):
    columns = columns_ref[...]
    rows = picked_rows(back_ref[...], 0, columns)
    fill_messages(send_ref, rows, 1, table_ref[...], columns)


def probs_kernel(back_ref, columns_ref, probs_ref):
    columns = columns_ref[...]
    found = picked_probs(back_ref[...], 0, columns)
    probs_ref[...] = jnp.concatenate(found + found, axis=1)


def last_kernel(back_ref, columns_ref, probs0_ref, probs_ref, final_ref):
    columns, back = columns_ref[...], back_ref[...]
    final_ref[...] = picked_rows(back, 1, columns)
    found = jnp.concatenate(picked_probs(back, 1, columns), axis=1)
    both = jnp.concatenate([probs0_ref[:, :OUTCOMES], found], axis=1)
    probs_ref[...] = both.T.astype(BF16)


def pack_kernel(place_ref, first_ref, second_ref, rest_ref, *packed_refs):
    ks, qs, ss, rs, lanes = first_ref.shape
    odd = lax.rem(place_ref[0], 2) == 1
    lane = iota((ss, rs, lanes), 2)
    low = lane < lanes // 2
    first_weight = jnp.where(low & jnp.logical_not(odd), 1.0, 2.0)
    second_weight = jnp.where(low | jnp.logical_not(odd), 2.0, 1.0)
    for d in range(qs):
        q = lax.rem(place_ref[1] + d, qs)
        for k in range(ks):
            parts = [
                (first_ref[k, q].astype(F32) * first_weight).reshape(ss * rs, lanes),
                (second_ref[k, q].astype(F32) * second_weight).reshape(ss * rs, lanes),
            ]
            rest = rest_ref[k, q].astype(F32)
            for s in range(0, ss, 2):
                one, two = rest[s], rest[s + 1]
                one = jnp.where(odd, pltpu.roll(one, lanes // 2, 1), one)
                two = jnp.where(odd, two, pltpu.roll(two, lanes // 2, 1))
                parts.append(jnp.where(low[0], one, two))
            packed_refs[d][k] = jnp.concatenate(parts, axis=0).astype(BF16)


def packed_blocks(place, environments):
    ks, qs, ss, rs, cs = environments.shape
    line = (ks, 10 * rs, LANES)
    tile = (ks, qs, ss, rs, LANES)

    def at(index):
        return pl.BlockSpec(tile, lambda i, place: (0, 0, 0, 0, lax.rem(index(place[0]), 4)))

    return pl.pallas_call(
        pack_kernel,
        out_shape=[shape(line, BF16)] * qs,
        grid_spec=pltpu.PrefetchScalarGridSpec(
            num_scalar_prefetch=1,
            grid=(1,),
            in_specs=[
                at(lambda z: lax.div(z + 1, 2)),
                at(lambda z: lax.div(z + 1, 2) + 1),
                at(lambda z: lax.div(z, 2) + 2 - 2 * lax.rem(z, 2)),
            ],
            out_specs=[pl.BlockSpec(line, lambda i, place: (0, 0, 0))] * qs,
        ),
        compiler_params=pltpu.CompilerParams(vmem_limit_bytes=VMEM_LIMIT),
    )(place, environments, environments, environments)


def unpack(part, blocks, env_ref):
    ds = 4
    rs = env_ref.shape[1] // (8 * ds)
    lane = iota((rs, LANES), 1)
    zero = jnp.zeros((rs, LANES), BF16)
    for z in range(8):
        odd, tile = z % 2, z // 2
        keep = (lane >= LANES // 2) if odd else (lane < LANES // 2)
        for d in range(ds):
            first = z * ds * rs + lax.rem(part + ds - d, ds) * rs
            rows = pl.ds(pl.multiple_of(first, rs), rs)
            block = blocks.at[z, d]

            def put(s, at, value):
                at %= 4
                env_ref[s, rows, at * LANES : (at + 1) * LANES] = value

            for s in range(OUTCOMES):
                put(s, tile + odd, block[s * rs : (s + 1) * rs, :])
                put(s, tile + odd + 1, block[(OUTCOMES + s) * rs : (OUTCOMES + s + 1) * rs, :])
                at = (2 * OUTCOMES + s // 2) * rs
                half = block[at : at + rs, :].astype(F32)
                if s % 2 != odd:
                    half = pltpu.roll(half, LANES // 2, 1)
                put(s, tile if odd else tile + 2, jnp.where(keep, half, 0.0).astype(BF16))
                put(s, tile + 3, zero)


def stage_kernel(count, k, place_ref, rows_ref, sites_hbm, *refs):
    packed_hbm, back_hbm = refs[:count], refs[count]
    packed, site_ref, back_ref, env_ref, picked_ref, in_sems, out_sems = refs[count + 1 :]
    row, part = place_ref[0], place_ref[1]
    slots, width = rows_ref.shape
    chunk = picked_ref.shape[0]
    depth = packed.shape[0]
    if count == 1:
        fetches = [pltpu.make_async_copy(packed_hbm[0], packed, in_sems.at[0])]
    else:
        fetches = [
            pltpu.make_async_copy(
                packed_hbm[i], packed.at[lax.rem(row + depth - i, depth)], in_sems.at[i]
            )
            for i in range(count)
        ]
    fetches.append(pltpu.make_async_copy(sites_hbm.at[k, part], site_ref, in_sems.at[count]))
    for fetch in fetches:
        fetch.start()
    for fetch in fetches[:count]:
        fetch.wait()
    unpack(part, packed, env_ref)
    for fetch in fetches[count:]:
        fetch.wait()

    messages = chunk // MSG
    cube = (messages, MSG, LANES)
    within = iota(cube, 1).reshape(chunk, LANES)
    diagonal = iota((chunk, LANES), 1) == within
    in_data = within[:, 0:1] < CAP
    sent = []
    for number, start in enumerate(range(0, slots, chunk)):
        at = slice(start, start + chunk)
        rows = rows_ref[at, :]
        front = rows[:, :LANES].astype(F32).reshape(cube)
        codes = jnp.broadcast_to(front[:, CAP : CAP + 1, :], cube).reshape(chunk, LANES)
        code = jnp.sum(jnp.where(diagonal, codes, 0.0), axis=1, keepdims=True)
        code = jnp.where(in_data, code, 0.0)
        weights = []
        for s in range(OUTCOMES):
            amplitudes = mm(rows, site_ref[:, width * s : width * (s + 1)])
            images = mm(amplitudes.astype(BF16), env_ref[s])
            weights.append(jnp.sum(images * amplitudes, axis=1, keepdims=True))
            chosen = code == (s + 1.0)
            if s == 0:
                picked_ref[...] = jnp.where(chosen, amplitudes, 0.0)
            else:
                picked_ref[...] = jnp.where(chosen, amplitudes, picked_ref[...])
        filled = code > 0.0
        total = jnp.where(filled, weights[0] + weights[1] + weights[2] + weights[3], 1.0)
        lines = jnp.zeros((chunk, LANES), F32)
        chosen_weight = jnp.ones((chunk, 1), F32)
        for s in range(OUTCOMES):
            prob = jnp.where(filled, weights[s] / total, 0.0)
            line = jnp.sum(jnp.where(diagonal, prob, 0.0).reshape(cube), axis=1, keepdims=True)
            line = jnp.broadcast_to(line, cube).reshape(chunk, LANES)
            lines = jnp.where(within == CAP + s, line, lines)
            chosen_weight = jnp.where(code == (s + 1.0), weights[s], chosen_weight)
        picked = picked_ref[...] * lax.rsqrt(chosen_weight / width)
        back_ref[at, :] = picked.astype(BF16)
        back_ref[at, :LANES] = jnp.where(in_data, picked[:, :LANES], lines).astype(BF16)
        copy = pltpu.make_async_copy(back_ref.at[at], back_hbm.at[at], out_sems.at[number])
        copy.start()
        sent.append(copy)
    for copy in sent:
        copy.wait()


def stage(k, place, rows, sites, packed):
    slots, width = rows.shape
    chunk = 16 * MSG
    count = len(packed)
    block = packed[0].shape[-3:]
    hbm, vmem = pl.BlockSpec(memory_space=pl.ANY), pl.BlockSpec(memory_space=pltpu.VMEM)
    return pl.pallas_call(
        functools.partial(stage_kernel, count, k),
        out_shape=shape((slots, width), BF16),
        in_specs=[pl.BlockSpec(memory_space=pltpu.SMEM), vmem] + [hbm] * (1 + count),
        out_specs=hbm,
        scratch_shapes=[
            pltpu.VMEM((8, *block), BF16),
            pltpu.VMEM(sites.shape[2:], BF16),
            pltpu.VMEM((slots, width), BF16),
            pltpu.VMEM((OUTCOMES, width, width), BF16),
            pltpu.VMEM((chunk, width), F32),
            pltpu.SemaphoreType.DMA((count + 1,)),
            pltpu.SemaphoreType.DMA((slots // chunk,)),
        ],
        compiler_params=pltpu.CompilerParams(vmem_limit_bytes=VMEM_LIMIT),
    )(place, near(rows), sites, *packed)


def local(vectors, sectors, outcomes, sites, environments):
    n, width = vectors.shape
    sector_total = sites.shape[1] * lax.axis_size("sector")
    parts, depth = lax.axis_size("part"), lax.axis_size("row")
    slots = sector_total * MSG
    place = jnp.stack([lax.axis_index("row"), lax.axis_index("part")]).astype(jnp.int32)

    blocks = packed_blocks(place, environments)
    blocks = [blocks[0]] + [
        lax.ppermute(blocks[d], "part", [(i, (i + d) % parts) for i in range(parts)])
        for d in range(1, parts)
    ]
    env0, env1 = (jnp.stack([block[k] for block in blocks]) for k in range(ORBITALS))
    env0, vectors = lax.optimization_barrier((env0, vectors))
    env0 = [lax.all_gather(env0, "row", axis=0)]
    send, table, columns = call(
        first_kernel,
        (shape((slots, width), BF16), pltpu.VMEM((8, n), F32), pltpu.VMEM((n, 8), F32)),
        vectors,
        sectors.T,
        outcomes.T,
    )

    def exchanged(messages):
        messages = messages.reshape(sector_total, MSG, width)
        messages = lax.all_to_all(
            messages, ("sector", "part"), split_axis=0, concat_axis=0, tiled=True
        )
        return messages.reshape(slots, width)

    back = exchanged(send)
    env1, _ = lax.optimization_barrier((env1, env0))
    env1 = [lax.all_gather(env1, "row", axis=0)]
    back = exchanged(stage(0, place, back, sites, env0))
    send = call(middle_kernel, shape((slots, width), BF16), back, table, columns)
    probs0 = call(probs_kernel, pltpu.VMEM((n, 8), F32), back, columns)
    back = exchanged(stage(1, place, exchanged(send), sites, env1))
    probs, final = call(
        last_kernel,
        (shape((ORBITALS * OUTCOMES, n), BF16), shape((n, width), BF16)),
        back,
        columns,
        probs0,
    )
    return (probs.T, final)


def solution(mesh):
    sector, section = mesh.devices.shape

    def whole(vectors, sectors, outcomes, sites, environments):
        parts = sites.shape[1] // sector
        fine = Mesh(
            mesh.devices.reshape(sector, section // parts, parts), ("sector", "row", "part")
        )
        split = P(("sector", "row", "part"), None)
        return jax.shard_map(
            local,
            mesh=fine,
            in_specs=(
                split,
                split,
                split,
                P(None, "sector", None, None),
                P(None, "sector", None, ("row", "part"), None),
            ),
            out_specs=(split, split),
            check_vma=False,
        )(vectors, sectors, outcomes, sites, environments)

    return whole
```

time: 296 us -> 170 us (0.57); the launches traced: 290 us -> 169 us
  local copies, waits for them, and re-layouts: 68.9 us -> 0.84 us
  matrix products: 58.9 us -> 0 us
  Pallas kernels: 0 us -> 30 us
  blocking collectives: 0 us -> 28.6 us
  waiting for transfers between devices: 89.5 us -> 66.1 us
  other arithmetic: 19.1 us -> 1.98 us
  starting transfers between devices: 38.9 us -> 27.2 us
    dot_general x4 -> x0, matrix products: 58.9 us -> none  [the longest x2 38.3 us: local(): jnp.einsum('iqcsb,qsbe->iqcse', rounded, environ_k, preferred_element_typ...]
    pallas_call x0 -> x7, Pallas kernels: none -> 30 us  [the longest x2 20.1 us: stage(): pl.pallas_call(functools.partial(stage_kernel, count, k), out_shape=shape...]
    all_to_all x0 -> x1, blocking collectives: none -> 28.6 us  [exchanged(): lax.all_to_all(messages, ('sector', 'part'), split_axis=0, concat_axis=0,...]
    reshape x10 -> x0, local copies, waits for them, and re-layouts: 27.6 us -> none  [the longest x2 23.9 us: local(): amplitudes.reshape(sector_count, per_device, slot_count, OUTCOMES, block_...]
    all_to_all x8 -> x3, waiting for transfers between devices: 63.6 us -> 45.7 us  [exchanged(): lax.all_to_all(messages, ('sector', 'part'), split_axis=0, concat_axis=0,...]
    all_to_all x8 -> x3, starting transfers between devices: 38.8 us -> 21.3 us  [exchanged(): lax.all_to_all(messages, ('sector', 'part'), split_axis=0, concat_axis=0,...]
    reduce_sum x6 -> x0, other arithmetic: 14.6 us -> none  [the longest x2 14.4 us: branch_results(): picked = jnp.sum(chosen_mask[..., None] * amplitudes, axis=-2)]
    scatter x4 -> x0, local copies, waits for them, and re-layouts: 12.8 us -> none  [the longest x2 6.9 us: local(): jnp.zeros((sector_total * capacity, block_width), jnp.bfloat16).at[slot_of]]
  transfers between devices with their start and end apart: 10 -> 8, of which waited for: 7 -> 7; matrix products, arithmetic and copies ran while one was open for 49% -> 1% of each run, Pallas kernels for 0% -> 3%
where the time goes in v2:
time: 170 us; the launch traced here: 169 us
  waiting for transfers between devices  66.1 us (39%)
  Pallas kernels  30 us (18%)
  blocking collectives  28.6 us (17%)
  starting transfers between devices  27.2 us (16%)
  between operations  14.1 us (8%)
  other arithmetic  1.98 us (1%)
    all_to_all x3, waiting for transfers between devices, exchanged(): lax.all_to_all(messages, ('sector', 'part'), split_axis=0, concat_axis=0,...  45.7 us
    all_to_all x1, blocking collectives, exchanged(): lax.all_to_all(messages, ('sector', 'part'), split_axis=0, concat_axis=0,...  28.6 us
    all_to_all x3, starting transfers between devices, exchanged(): lax.all_to_all(messages, ('sector', 'part'), split_axis=0, concat_axis=0,...  21.3 us
    pallas_call x2, Pallas kernels, stage(): pl.pallas_call(functools.partial(stage_kernel, count, k), out_shape=shape...  20.1 us
    all_gather x1, waiting for transfers between devices, local(): env1 = [lax.all_gather(env1, 'row', axis=0)]  9.87 us
    all_gather x1, waiting for transfers between devices, local(): env0 = [lax.all_gather(env0, 'row', axis=0)]  8.59 us
    pallas_call x4, Pallas kernels, call(): pl.pallas_call(body, out_shape=outs, in_specs=[vmem] * len(args), out_spe...  7.28 us
    ppermute x3, starting transfers between devices, local(): lax.ppermute(blocks[d], 'part', [(i, (i + d) % parts) for i in range(part...  5.81 us
  transfers between devices with their start and end apart: 8, of which 7 were waited for; matrix products, arithmetic and copies ran while one was open for 1% of the time, Pallas kernels for 3%

profile of v2, /device:TPU:1, one launch (start us, length us, event | category | flops | bytes accessed | tf_op | source)
XLA Modules:
  0.0 168.9 jit_solution(6708110853718224217)
XLA Ops:
  7.2 0.6 pad_add_fusion.place_ref
  7.8 2.6 %shard_map.68 = (bf16[2,160,128]{2,1,0:T(8,128)(2,1)}, bf16[2,160,128]{2,1,0:T(8,128)(2,1)}, bf16[2,160,128]{2,1,0:T(8,128)(2,1)}, bf16[2,160,128]{2,1,0:T(8,128)(2,1)}) custom-call(s32[2]{0:T(128)} %pad_add_fusion.place_ref, bf16[2,4,4,16,512]{4,3,2,1,0:T(8,128)(2,1)} %rest_ref.1, bf16[2,4,4,16,512]{4,3,2,1,0:T(8,128)(2,1)} %rest_ref.1, ...), custom_call_target="tpu_custom_call" | custom-call | tf_op jit(solution)/shard_map/pallas_call | solution.py:174
  10.5 2.1 %collective-permute-start = (bf16[2,160,128]{2,1,0:T(8,128)(2,1)}, bf16[2,160,128]{2,1,0:T(8,128)(2,1)S(1)}, u32[]{:S(2)}, u32[]{:S(2)}) collective-permute-start(bf16[2,160,128]{2,1,0:T(8,128)(2,1)} %get-tuple-element.15), channel_id=1, source_target_pairs={{0,1},{1,2},{2,3},{3,0},{4,5},{5,6},{6,7},{7,4},{8,9},{9,10},{10,1... | collective-permute-start | bytes 245768 | tf_op jit(solution)/shard_map/ppermute | solution.py:320
  12.6 2.6 %collective-permute-start.1 = (bf16[2,160,128]{2,1,0:T(8,128)(2,1)}, bf16[2,160,128]{2,1,0:T(8,128)(2,1)S(1)}, u32[]{:S(2)}, u32[]{:S(2)}) collective-permute-start(bf16[2,160,128]{2,1,0:T(8,128)(2,1)} %get-tuple-element.16), channel_id=1, source_target_pairs={{0,2},{1,3},{2,0},{3,1},{4,6},{5,7},{6,4},{7,5},{8,10},{9,11},{10,... | collective-permute-start | bytes 245768 | tf_op jit(solution)/shard_map/ppermute | solution.py:320
  15.2 1.1 collective-permute-start.2
  16.3 0.8 fusion
  17.1 1.6 collective-permute-done.1
  19.0 0.7 pad_maximum_fusion
  19.8 2.2 %shard_map.69 = (bf16[1280,512]{1,0:T(8,128)(2,1)}, f32[8,384]{1,0:T(8,128)S(1)}, f32[384,8]{1,0:T(8,128)S(1)}) custom-call(bf16[384,512]{1,0:T(8,128)(2,1)S(1)} %copy-done, s32[2,384]{1,0:T(2,128)S(1)} %bitcast.20, s32[2,384]{1,0:T(2,128)S(1)} %bitcast.21), custom_call_target="tpu_custom_call" | custom-call | tf_op jit(solution)/shard_map/pallas_call | solution.py:32
  21.9 28.6 %all_to_all.20 = bf16[32,40,512]{2,1,0:T(8,128)(2,1)S(1)} all-to-all(bf16[32,40,512]{2,1,0:T(8,128)(2,1)} %bitcast.27), channel_id=1, replica_groups=mesh['sector'=8,'row'=8,'part'=4] {'sector','part'}, dimensions={0} | all-to-all | bytes 2621440 | tf_op jit(solution)/shard_map/all_to_all | solution.py:336
  50.6 8.6 %all-gather.5.cloned.1.call-done = bf16[32,160,128]{2,1,0:T(8,128)(2,1)} async-done(((bf16[4,160,128]{2,1,0:T(8,128)(2,1)}), bf16[32,160,128]{2,1,0:T(8,128)(2,1)}) %all-gather.5.cloned.1.call-update) | async-done | bytes 1310736 | tf_op jit(solution)/shard_map/all_gather | solution.py:325
  59.2 10.0 %shard_map.70 = bf16[1280,512]{1,0:T(8,128)(2,1)} custom-call(s32[2]{0:T(128)} %pad_add_fusion.place_ref, bf16[1280,512]{1,0:T(8,128)(2,1)S(1)} %bitcast.18, bf16[2,4,512,2048]{3,2,1,0:T(8,128)(2,1)} %sites_hbm.3, bf16[8,4,160,128]{3,2,1,0:T(8,128)(2,1)} %bitcast.26), custom_call_target="tpu_custom_call" | custom-call | tf_op jit(solution)/shard_map/pallas_call | solution.py:293
  69.2 11.4 %all-to-all-start.1 = ((bf16[32,40,512]{2,1,0:T(8,128)(2,1)}), bf16[32,40,512]{2,1,0:T(8,128)(2,1)S(1)}, u32[]{:S(2)}, u32[]{:S(2)}) async-start(bf16[32,40,512]{2,1,0:T(8,128)(2,1)} %bitcast.22), calls=%async_computation.1 | async-start | bytes 2621440 | tf_op jit(solution)/shard_map/all_to_all | solution.py:336
  80.7 0.7 pad_maximum_fusion.1
  81.4 18.1 %all-to-all-done.1 = bf16[32,40,512]{2,1,0:T(8,128)(2,1)S(1)} async-done(((bf16[32,40,512]{2,1,0:T(8,128)(2,1)}), bf16[32,40,512]{2,1,0:T(8,128)(2,1)S(1)}, u32[]{:S(2)}, u32[]{:S(2)}) %all-to-all-start.1) | async-done | bytes 1310752 | tf_op jit(solution)/shard_map/all_to_all | solution.py:336
  99.5 2.7 %shard_map.71 = bf16[1280,512]{1,0:T(8,128)(2,1)} custom-call(bf16[1280,512]{1,0:T(8,128)(2,1)S(1)} %bitcast.15, f32[8,384]{1,0:T(8,128)S(1)} %get-tuple-element.21.table_ref, f32[384,8]{1,0:T(8,128)S(1)} %get-tuple-element.22.columns_ref), custom_call_target="tpu_custom_call" | custom-call | tf_op jit(solution)/shard_map/pallas_call | solution.py:32
  102.2 5.0 %all-to-all-start.2 = ((bf16[32,40,512]{2,1,0:T(8,128)(2,1)}), bf16[32,40,512]{2,1,0:T(8,128)(2,1)S(1)}, u32[]{:S(2)}, u32[]{:S(2)}) async-start(bf16[32,40,512]{2,1,0:T(8,128)(2,1)} %bitcast.24), calls=%async_computation.2 | async-start | bytes 2621440 | tf_op jit(solution)/shard_map/all_to_all | solution.py:336
  107.3 9.9 %all-gather.7.cloned.1.call-done = bf16[32,160,128]{2,1,0:T(8,128)(2,1)} async-done(((bf16[4,160,128]{2,1,0:T(8,128)(2,1)}), bf16[32,160,128]{2,1,0:T(8,128)(2,1)}) %all-gather.7.cloned.1.call-update) | async-done | bytes 1310736 | tf_op jit(solution)/shard_map/all_gather | solution.py:343
  117.2 9.1 %all-to-all-done.2 = bf16[32,40,512]{2,1,0:T(8,128)(2,1)S(1)} async-done(((bf16[32,40,512]{2,1,0:T(8,128)(2,1)}), bf16[32,40,512]{2,1,0:T(8,128)(2,1)S(1)}, u32[]{:S(2)}, u32[]{:S(2)}) %all-to-all-start.2) | async-done | bytes 1310752 | tf_op jit(solution)/shard_map/all_to_all | solution.py:336
  126.3 10.0 %shard_map.72 = bf16[1280,512]{1,0:T(8,128)(2,1)} custom-call(s32[2]{0:T(128)} %pad_add_fusion.place_ref, bf16[1280,512]{1,0:T(8,128)(2,1)S(1)} %bitcast.17, bf16[2,4,512,2048]{3,2,1,0:T(8,128)(2,1)} %sites_hbm.3, bf16[8,4,160,128]{3,2,1,0:T(8,128)(2,1)} %bitcast.25), custom_call_target="tpu_custom_call" | custom-call | tf_op jit(solution)/shard_map/pallas_call | solution.py:293
  136.3 4.9 %all-to-all-start.3 = ((bf16[32,40,512]{2,1,0:T(8,128)(2,1)}), bf16[32,40,512]{2,1,0:T(8,128)(2,1)S(1)}, u32[]{:S(2)}, u32[]{:S(2)}) async-start(bf16[32,40,512]{2,1,0:T(8,128)(2,1)} %bitcast.23), calls=%async_computation.3 | async-start | bytes 2621440 | tf_op jit(solution)/shard_map/all_to_all | solution.py:336
  141.2 0.5 shard_map.73.probs0_ref
  141.7 18.5 %all-to-all-done.3 = bf16[32,40,512]{2,1,0:T(8,128)(2,1)S(1)} async-done(((bf16[32,40,512]{2,1,0:T(8,128)(2,1)}), bf16[32,40,512]{2,1,0:T(8,128)(2,1)S(1)}, u32[]{:S(2)}, u32[]{:S(2)}) %all-to-all-start.3) | async-done | bytes 1310752 | tf_op jit(solution)/shard_map/all_to_all | solution.py:336
  160.2 1.9 %shard_map.74 = (bf16[8,384]{1,0:T(8,128)(2,1)}, bf16[384,512]{1,0:T(8,128)(2,1)}) custom-call(bf16[1280,512]{1,0:T(8,128)(2,1)S(1)} %bitcast.19, f32[384,8]{1,0:T(8,128)S(1)} %get-tuple-element.22.columns_ref, f32[384,8]{1,0:T(8,128)S(1)} %shard_map.73.probs0_ref), custom_call_target="tpu_custom_call" | custom-call | tf_op jit(solution)/shard_map/pallas_call | solution.py:32
  (15 shorter events, 0.4 us)
Async XLA Ops:
  7.2 52.0 %all-gather.5.cloned.1.call-start = ((), (), s32[]{:S(2)}) async-start(), calls=%async_computation.4 | async-start | bytes 1474560 | tf_op jit(solution)/shard_map/all_gather | solution.py:325
  7.8 11.9 %copy-start = (bf16[384,512]{1,0:T(8,128)(2,1)S(1)}, bf16[384,512]{1,0:T(8,128)(2,1)}, u32[]{:S(2)}) copy-start(bf16[384,512]{1,0:T(8,128)(2,1)} %vec_ref) | copy-start | bytes 1179652
  7.8 11.9 %copy-start.1 = (s32[384,2]{0,1:T(2,128)S(1)}, s32[384,2]{0,1:T(2,128)}, u32[]{:S(2)}) copy-start(s32[384,2]{0,1:T(2,128)} %param.6) | copy-start | bytes 9220
  7.8 11.9 %copy-start.2 = (s32[384,2]{0,1:T(2,128)S(1)}, s32[384,2]{0,1:T(2,128)}, u32[]{:S(2)}) copy-start(s32[384,2]{0,1:T(2,128)} %param.7) | copy-start | bytes 9220
  10.5 6.6 %collective-permute-start = (bf16[2,160,128]{2,1,0:T(8,128)(2,1)}, bf16[2,160,128]{2,1,0:T(8,128)(2,1)S(1)}, u32[]{:S(2)}, u32[]{:S(2)}) collective-permute-start(bf16[2,160,128]{2,1,0:T(8,128)(2,1)} %get-tuple-element.15), channel_id=1, source_target_pairs={{0,1},{1,2},{2,3},{3,0},{4,5},{5,6},{6,7},{7,4},{8,9},{9,10},{10,1... | collective-permute-start | bytes 245768 | tf_op jit(solution)/shard_map/ppermute | solution.py:320
  12.6 6.1 %collective-permute-start.1 = (bf16[2,160,128]{2,1,0:T(8,128)(2,1)}, bf16[2,160,128]{2,1,0:T(8,128)(2,1)S(1)}, u32[]{:S(2)}, u32[]{:S(2)}) collective-permute-start(bf16[2,160,128]{2,1,0:T(8,128)(2,1)} %get-tuple-element.16), channel_id=1, source_target_pairs={{0,2},{1,3},{2,0},{3,1},{4,6},{5,7},{6,4},{7,5},{8,10},{9,11},{10,... | collective-permute-start | bytes 245768 | tf_op jit(solution)/shard_map/ppermute | solution.py:320
  15.2 3.8 %collective-permute-start.2 = (bf16[2,160,128]{2,1,0:T(8,128)(2,1)}, bf16[2,160,128]{2,1,0:T(8,128)(2,1)S(1)}, u32[]{:S(2)}, u32[]{:S(2)}) collective-permute-start(bf16[2,160,128]{2,1,0:T(8,128)(2,1)} %get-tuple-element.17), channel_id=1, source_target_pairs={{0,3},{1,0},{2,1},{3,2},{4,7},{5,4},{6,5},{7,6},{8,11},{9,8},{10,9... | collective-permute-start | bytes 245768 | tf_op jit(solution)/shard_map/ppermute | solution.py:320
  69.2 30.3 %all-to-all-start.1 = ((bf16[32,40,512]{2,1,0:T(8,128)(2,1)}), bf16[32,40,512]{2,1,0:T(8,128)(2,1)S(1)}, u32[]{:S(2)}, u32[]{:S(2)}) async-start(bf16[32,40,512]{2,1,0:T(8,128)(2,1)} %bitcast.22), calls=%async_computation.1 | async-start | bytes 2621440 | tf_op jit(solution)/shard_map/all_to_all | solution.py:336
  80.6 36.6 %all-gather.7.cloned.1.call-start = ((), (), s32[]{:S(2)}) async-start(), calls=%async_computation.5 | async-start | bytes 1474560 | tf_op jit(solution)/shard_map/all_gather | solution.py:343
  102.2 24.0 %all-to-all-start.2 = ((bf16[32,40,512]{2,1,0:T(8,128)(2,1)}), bf16[32,40,512]{2,1,0:T(8,128)(2,1)S(1)}, u32[]{:S(2)}, u32[]{:S(2)}) async-start(bf16[32,40,512]{2,1,0:T(8,128)(2,1)} %bitcast.24), calls=%async_computation.2 | async-start | bytes 2621440 | tf_op jit(solution)/shard_map/all_to_all | solution.py:336
  136.3 23.9 %all-to-all-start.3 = ((bf16[32,40,512]{2,1,0:T(8,128)(2,1)}), bf16[32,40,512]{2,1,0:T(8,128)(2,1)S(1)}, u32[]{:S(2)}, u32[]{:S(2)}) async-start(bf16[32,40,512]{2,1,0:T(8,128)(2,1)} %bitcast.23), calls=%async_computation.3 | async-start | bytes 2621440 | tf_op jit(solution)/shard_map/all_to_all | solution.py:336
Sparse Core Ops, SparseCore 0:
  19.8 39.2 all-gather.4
  83.8 33.3 all-gather.6

commit v3 on v2

--- a/solution.py
+++ b/solution.py
@@ -13,7 +13,9 @@
 CAP = 36
 MSG = 40
 LANES = 128
+PARTS = 4
 VMEM_LIMIT = 56 * 1024 * 1024
+PACK_LIMIT = 10 * 1024 * 1024
 
 F32 = jnp.float32
 BF16 = jnp.bfloat16
@@ -140,36 +142,42 @@
     probs_ref[...] = both.T.astype(BF16)
 
 
+def row_and_part(place):
+    return lax.div(place, PARTS), lax.rem(place, PARTS)
+
+
 def pack_kernel(place_ref, first_ref, second_ref, rest_ref, *packed_refs):
-    ks, qs, ss, rs, lanes = first_ref.shape
-    odd = lax.rem(place_ref[0], 2) == 1
+    _, qs, ss, rs, lanes = first_ref.shape
+    row, part = row_and_part(place_ref[0])
+    odd = lax.rem(row, 2) == 1
     lane = iota((ss, rs, lanes), 2)
     low = lane < lanes // 2
     first_weight = jnp.where(low & jnp.logical_not(odd), 1.0, 2.0)
     second_weight = jnp.where(low | jnp.logical_not(odd), 2.0, 1.0)
     for d in range(qs):
-        q = lax.rem(place_ref[1] + d, qs)
-        for k in range(ks):
-            parts = [
-                (first_ref[k, q].astype(F32) * first_weight).reshape(ss * rs, lanes),
-                (second_ref[k, q].astype(F32) * second_weight).reshape(ss * rs, lanes),
-            ]
-            rest = rest_ref[k, q].astype(F32)
-            for s in range(0, ss, 2):
-                one, two = rest[s], rest[s + 1]
-                one = jnp.where(odd, pltpu.roll(one, lanes // 2, 1), one)
-                two = jnp.where(odd, two, pltpu.roll(two, lanes // 2, 1))
-                parts.append(jnp.where(low[0], one, two))
-            packed_refs[d][k] = jnp.concatenate(parts, axis=0).astype(BF16)
-
-
-def packed_blocks(place, environments):
-    ks, qs, ss, rs, cs = environments.shape
-    line = (ks, 10 * rs, LANES)
-    tile = (ks, qs, ss, rs, LANES)
+        q = lax.rem(part + d, qs)
+        parts = [
+            (first_ref[0, q].astype(F32) * first_weight).reshape(ss * rs, lanes),
+            (second_ref[0, q].astype(F32) * second_weight).reshape(ss * rs, lanes),
+        ]
+        rest = rest_ref[0, q].astype(F32)
+        for s in range(0, ss, 2):
+            one, two = rest[s], rest[s + 1]
+            one = jnp.where(odd, pltpu.roll(one, lanes // 2, 1), one)
+            two = jnp.where(odd, two, pltpu.roll(two, lanes // 2, 1))
+            parts.append(jnp.where(low[0], one, two))
+        packed_refs[d][...] = jnp.concatenate(parts, axis=0).astype(BF16)
+
+
+def packed_blocks(place, environments, k):
+    _, qs, ss, rs, cs = environments.shape
+    line = (10 * rs, LANES)
 
     def at(index):
-        return pl.BlockSpec(tile, lambda i, place: (0, 0, 0, 0, lax.rem(index(place[0]), 4)))
+        def place_of(i, place):
+            return (k, 0, 0, 0, lax.rem(index(row_and_part(place[0])[0]), 4))
+
+        return pl.BlockSpec((1, qs, ss, rs, LANES), place_of)
 
     return pl.pallas_call(
         pack_kernel,
@@ -182,9 +190,9 @@
                 at(lambda z: lax.div(z + 1, 2) + 1),
                 at(lambda z: lax.div(z, 2) + 2 - 2 * lax.rem(z, 2)),
             ],
-            out_specs=[pl.BlockSpec(line, lambda i, place: (0, 0, 0))] * qs,
+            out_specs=[pl.BlockSpec(line, lambda i, place: (0, 0))] * qs,
         ),
-        compiler_params=pltpu.CompilerParams(vmem_limit_bytes=VMEM_LIMIT),
+        compiler_params=pltpu.CompilerParams(vmem_limit_bytes=PACK_LIMIT),
     )(place, environments, environments, environments)
 
 
@@ -216,30 +224,35 @@
                 put(s, tile + 3, zero)
 
 
-def stage_kernel(count, k, place_ref, rows_ref, sites_hbm, *refs):
-    packed_hbm, back_hbm = refs[:count], refs[count]
-    packed, site_ref, back_ref, env_ref, picked_ref, in_sems, out_sems = refs[count + 1 :]
-    row, part = place_ref[0], place_ref[1]
+def stage_kernel(
+    k,
+    place_ref,
+    rows_ref,
+    sites_hbm,
+    packed_hbm,
+    back_hbm,
+    packed,
+    site_ref,
+    back_ref,
+    env_ref,
+    picked_ref,
+    in_sems,
+    out_sems,
+):
+    row, part = row_and_part(place_ref[0])
     slots, width = rows_ref.shape
     chunk = picked_ref.shape[0]
-    depth = packed.shape[0]
-    if count == 1:
-        fetches = [pltpu.make_async_copy(packed_hbm[0], packed, in_sems.at[0])]
-    else:
-        fetches = [
-            pltpu.make_async_copy(
-                packed_hbm[i], packed.at[lax.rem(row + depth - i, depth)], in_sems.at[i]
-            )
-            for i in range(count)
-        ]
-    fetches.append(pltpu.make_async_copy(sites_hbm.at[k, part], site_ref, in_sems.at[count]))
-    for fetch in fetches:
-        fetch.start()
-    for fetch in fetches[:count]:
-        fetch.wait()
-    unpack(part, packed, env_ref)
-    for fetch in fetches[count:]:
-        fetch.wait()
+    gathered = pltpu.make_async_copy(packed_hbm, packed, in_sems.at[OUTCOMES])
+    sites = [
+        pltpu.make_async_copy(
+            sites_hbm.at[k, part, :, width * s : width * (s + 1)], site_ref.at[s], in_sems.at[s]
+        )
+        for s in range(OUTCOMES)
+    ]
+    sites[0].start()
+    gathered.start()
+    for s in range(1, OUTCOMES):
+        sites[s].start()
 
     messages = chunk // MSG
     cube = (messages, MSG, LANES)
@@ -256,7 +269,12 @@
         code = jnp.where(in_data, code, 0.0)
         weights = []
         for s in range(OUTCOMES):
-            amplitudes = mm(rows, site_ref[:, width * s : width * (s + 1)])
+            if number == 0:
+                sites[s].wait()
+            amplitudes = mm(rows, site_ref[s])
+            if number == 0 and s == 0:
+                gathered.wait()
+                unpack(part, packed, env_ref)
             images = mm(amplitudes.astype(BF16), env_ref[s])
             weights.append(jnp.sum(images * amplitudes, axis=1, keepdims=True))
             chosen = code == (s + 1.0)
@@ -291,38 +309,41 @@
     block = packed[0].shape[-3:]
     hbm, vmem = pl.BlockSpec(memory_space=pl.ANY), pl.BlockSpec(memory_space=pltpu.VMEM)
     return pl.pallas_call(
-        functools.partial(stage_kernel, count, k),
+        functools.partial(stage_kernel, k),
         out_shape=shape((slots, width), BF16),
-        in_specs=[pl.BlockSpec(memory_space=pltpu.SMEM), vmem] + [hbm] * (1 + count),
+        in_specs=[pl.BlockSpec(memory_space=pltpu.SMEM), vmem, hbm, hbm],
         out_specs=hbm,
         scratch_shapes=[
-            pltpu.VMEM((8, *block), BF16),
-            pltpu.VMEM(sites.shape[2:], BF16),
+            pltpu.VMEM(packed.shape, BF16),
+            pltpu.VMEM((OUTCOMES, width, width), BF16),
             pltpu.VMEM((slots, width), BF16),
             pltpu.VMEM((OUTCOMES, width, width), BF16),
             pltpu.VMEM((chunk, width), F32),
-            pltpu.SemaphoreType.DMA((count + 1,)),
+            pltpu.SemaphoreType.DMA((OUTCOMES + 1,)),
             pltpu.SemaphoreType.DMA((slots // chunk,)),
         ],
         compiler_params=pltpu.CompilerParams(vmem_limit_bytes=VMEM_LIMIT),
-    )(place, near(rows), sites, *packed)
+    )(place, near(rows), sites, packed)
 
 
 def local(vectors, sectors, outcomes, sites, environments):
     n, width = vectors.shape
     sector_total = sites.shape[1] * lax.axis_size("sector")
-    parts, depth = lax.axis_size("part"), lax.axis_size("row")
     slots = sector_total * MSG
-    place = jnp.stack([lax.axis_index("row"), lax.axis_index("part")]).astype(jnp.int32)
-
-    blocks = packed_blocks(place, environments)
-    blocks = [blocks[0]] + [
-        lax.ppermute(blocks[d], "part", [(i, (i + d) % parts) for i in range(parts)])
-        for d in range(1, parts)
-    ]
-    env0, env1 = (jnp.stack([block[k] for block in blocks]) for k in range(ORBITALS))
-    env0, vectors = lax.optimization_barrier((env0, vectors))
-    env0 = [lax.all_gather(env0, "row", axis=0)]
+    place = lax.axis_index(("row", "part")).astype(jnp.int32).reshape(1)
+
+    def own_blocks(environments, k):
+        blocks = packed_blocks(place, environments, k)
+        blocks = [blocks[0]] + [
+            lax.ppermute(blocks[d], "part", [(i, (i + d) % PARTS) for i in range(PARTS)])
+            for d in range(1, PARTS)
+        ]
+        return jnp.stack(blocks)
+
+    env0 = own_blocks(environments, 0)
+    env0, environments = lax.optimization_barrier((env0, environments))
+    env0 = lax.all_gather(env0, "row", axis=0)
+    env1, vectors = lax.optimization_barrier((own_blocks(environments, 1), vectors))
     send, table, columns = call(
         first_kernel,
         (shape((slots, width), BF16), pltpu.VMEM((8, n), F32), pltpu.VMEM((n, 8), F32)),
@@ -339,8 +360,8 @@
         return messages.reshape(slots, width)
 
     back = exchanged(send)
-    env1, _ = lax.optimization_barrier((env1, env0))
-    env1 = [lax.all_gather(env1, "row", axis=0)]
+    env1, env0 = lax.optimization_barrier((env1, env0))
+    env1 = lax.all_gather(env1, "row", axis=0)
     back = exchanged(stage(0, place, back, sites, env0))
     send = call(middle_kernel, shape((slots, width), BF16), back, table, columns)
     probs0 = call(probs_kernel, pltpu.VMEM((n, 8), F32), back, columns)
@@ -359,9 +380,8 @@
     sector, section = mesh.devices.shape
 
     def whole(vectors, sectors, outcomes, sites, environments):
-        parts = sites.shape[1] // sector
         fine = Mesh(
-            mesh.devices.reshape(sector, section // parts, parts), ("sector", "row", "part")
+            mesh.devices.reshape(sector, section // PARTS, PARTS), ("sector", "row", "part")
         )
         split = P(("sector", "row", "part"), None)
         return jax.shard_map(

time: 170 us -> 166 us (0.976)
  blocking collectives: 28.6 us -> 0 us
  waiting for transfers between devices: 66.1 us -> 82.1 us
  starting transfers between devices: 27.2 us -> 39.8 us
  Pallas kernels: 30 us -> 27.1 us
    all_to_all x1 -> x0, blocking collectives: 28.6 us -> none  [exchanged(): lax.all_to_all(messages, ('sector', 'part'), split_axis=0, concat_axis=0,...]
    all_gather x2, waiting for transfers between devices: 18.5 us -> 30.5 us  [the longest x1 20.7 us: local(): env0 = lax.all_gather(env0, 'row', axis=0)]
    all_to_all x3 -> x4, starting transfers between devices: 21.3 us -> 30.4 us  [exchanged(): lax.all_to_all(messages, ('sector', 'part'), split_axis=0, concat_axis=0,...]
    ppermute x3 -> x6, starting transfers between devices: 5.81 us -> 9.25 us  [own_blocks(): lax.ppermute(blocks[d], 'part', [(i, (i + d) % PARTS) for i in range(PART...]
    ppermute x3 -> x6, waiting for transfers between devices: 1.9 us -> 5.11 us  [own_blocks(): lax.ppermute(blocks[d], 'part', [(i, (i + d) % PARTS) for i in range(PART...]
    pallas_call x1 -> x2, Pallas kernels: 2.64 us -> 0.29 us  [packed_blocks(): pl.pallas_call(pack_kernel, out_shape=[shape(line, BF16)] * qs, grid_spec...]
    all_to_all x3 -> x4, waiting for transfers between devices: 45.7 us -> 45.8 us  [exchanged(): lax.all_to_all(messages, ('sector', 'part'), split_axis=0, concat_axis=0,...]
  transfers between devices with their start and end apart: 8 -> 12, of which waited for: 7 -> 10; matrix products, arithmetic and copies ran while one was open for 1% -> 0% of each run, Pallas kernels for 3% -> 3%
where the time goes in v3:
time: 166 us
  waiting for transfers between devices  82.1 us (49%)
  starting transfers between devices  39.8 us (24%)
  Pallas kernels  27.1 us (16%)
  between operations  14.2 us (9%)
    all_to_all x4, waiting for transfers between devices, exchanged(): lax.all_to_all(messages, ('sector', 'part'), split_axis=0, concat_axis=0,...  45.8 us
    all_to_all x4, starting transfers between devices, exchanged(): lax.all_to_all(messages, ('sector', 'part'), split_axis=0, concat_axis=0,...  30.4 us
    all_gather x1, waiting for transfers between devices, local(): env0 = lax.all_gather(env0, 'row', axis=0)  20.7 us
    pallas_call x2, Pallas kernels, stage(): pl.pallas_call(functools.partial(stage_kernel, k), out_shape=shape((slots...  19.6 us
    all_gather x1, waiting for transfers between devices, local(): env1 = lax.all_gather(env1, 'row', axis=0)  9.82 us
    ppermute x6, starting transfers between devices, own_blocks(): lax.ppermute(blocks[d], 'part', [(i, (i + d) % PARTS) for i in range(PART...  9.25 us
    pallas_call x4, Pallas kernels, call(): pl.pallas_call(body, out_shape=outs, in_specs=[vmem] * len(args), out_spe...  7.26 us
    ppermute x6, waiting for transfers between devices, own_blocks(): lax.ppermute(blocks[d], 'part', [(i, (i + d) % PARTS) for i in range(PART...  5.11 us
  transfers between devices with their start and end apart: 12, of which 10 were waited for; matrix products, arithmetic and copies ran while one was open for 0% of the time, Pallas kernels for 3%

profile of v3, /device:TPU:1, one launch (start us, length us, event | category | flops | bytes accessed | tf_op | source)
XLA Modules:
  0.0 165.7 jit_solution(3118760279634331405)
XLA Ops:
  7.2 1.0 copy-done
  8.4 2.2 %collective-permute-start = (bf16[160,128]{1,0:T(8,128)(2,1)S(1)}, bf16[160,128]{1,0:T(8,128)(2,1)S(1)}, u32[]{:S(2)}, u32[]{:S(2)}) collective-permute-start(bf16[160,128]{1,0:T(8,128)(2,1)S(1)} %get-tuple-element.22), channel_id=1, source_target_pairs={{0,1},{1,2},{2,3},{3,0},{4,5},{5,6},{6,7},{7,4},{8,9},{9,10},{10,1... | collective-permute-start | bytes 122888 | tf_op jit(solution)/shard_map/ppermute | solution.py:338
  10.6 2.6 %collective-permute-start.1 = (bf16[160,128]{1,0:T(8,128)(2,1)S(1)}, bf16[160,128]{1,0:T(8,128)(2,1)S(1)}, u32[]{:S(2)}, u32[]{:S(2)}) collective-permute-start(bf16[160,128]{1,0:T(8,128)(2,1)S(1)} %get-tuple-element.23), channel_id=1, source_target_pairs={{0,2},{1,3},{2,0},{3,1},{4,6},{5,7},{6,4},{7,5},{8,10},{9,11},{10,... | collective-permute-start | bytes 122888 | tf_op jit(solution)/shard_map/ppermute | solution.py:338
  13.3 1.1 collective-permute-start.2
  14.3 0.8 collective-permute-done.1
  15.1 1.3 collective-permute-done.2
  17.4 3.2 %collective-permute-start.4 = (bf16[160,128]{1,0:T(8,128)(2,1)S(1)}, bf16[160,128]{1,0:T(8,128)(2,1)S(1)}, u32[]{:S(2)}, u32[]{:S(2)}) collective-permute-start(bf16[160,128]{1,0:T(8,128)(2,1)S(1)} %get-tuple-element.28), channel_id=1, source_target_pairs={{0,2},{1,3},{2,0},{3,1},{4,6},{5,7},{6,4},{7,5},{8,10},{9,11},{10,... | collective-permute-start | bytes 122888 | tf_op jit(solution)/shard_map/ppermute | solution.py:338
  20.7 0.8 collective-permute-done.3
  21.4 0.9 collective-permute-done.4
  22.4 1.3 collective-permute-done.5
  24.4 2.2 %shard_map.70 = (bf16[1280,512]{1,0:T(8,128)(2,1)}, f32[8,384]{1,0:T(8,128)S(1)}, f32[384,8]{1,0:T(8,128)S(1)}) custom-call(bf16[384,512]{1,0:T(8,128)(2,1)S(1)} %copy-done.2, s32[2,384]{1,0:T(2,128)S(1)} %bitcast.29, s32[2,384]{1,0:T(2,128)S(1)} %bitcast.30), custom_call_target="tpu_custom_call" | custom-call | tf_op jit(solution)/shard_map/pallas_call | solution.py:34
  26.6 9.2 %all-to-all-start = ((bf16[32,40,512]{2,1,0:T(8,128)(2,1)}), bf16[32,40,512]{2,1,0:T(8,128)(2,1)S(1)}, u32[]{:S(2)}, u32[]{:S(2)}) async-start(bf16[32,40,512]{2,1,0:T(8,128)(2,1)} %bitcast.36), calls=%async_computation | async-start | bytes 2621440 | tf_op jit(solution)/shard_map/all_to_all | solution.py:357
  35.8 20.7 %all-gather.5.cloned.1.call-done = bf16[32,160,128]{2,1,0:T(8,128)(2,1)} async-done(((bf16[4,160,128]{2,1,0:T(8,128)(2,1)}), bf16[32,160,128]{2,1,0:T(8,128)(2,1)}) %all-gather.5.cloned.1.call-update) | async-done | bytes 1310736 | tf_op jit(solution)/shard_map/all_gather | solution.py:345
  56.5 9.8 %shard_map.71 = bf16[1280,512]{1,0:T(8,128)(2,1)} custom-call(s32[1]{0:T(128)} %bitcast.place_ref, bf16[1280,512]{1,0:T(8,128)(2,1)S(1)} %bitcast.25, bf16[2,4,512,2048]{3,2,1,0:T(8,128)(2,1)} %sites_hbm.3, bf16[8,4,160,128]{3,2,1,0:T(8,128)(2,1)} %bitcast.34), custom_call_target="tpu_custom_call" | custom-call | tf_op jit(solution)/shard_map/pallas_call | solution.py:311
  66.3 11.5 %all-to-all-start.1 = ((bf16[32,40,512]{2,1,0:T(8,128)(2,1)}), bf16[32,40,512]{2,1,0:T(8,128)(2,1)S(1)}, u32[]{:S(2)}, u32[]{:S(2)}) async-start(bf16[32,40,512]{2,1,0:T(8,128)(2,1)} %bitcast.31), calls=%async_computation.1 | async-start | bytes 2621440 | tf_op jit(solution)/shard_map/all_to_all | solution.py:357
  78.5 18.1 %all-to-all-done.1 = bf16[32,40,512]{2,1,0:T(8,128)(2,1)S(1)} async-done(((bf16[32,40,512]{2,1,0:T(8,128)(2,1)}), bf16[32,40,512]{2,1,0:T(8,128)(2,1)S(1)}, u32[]{:S(2)}, u32[]{:S(2)}) %all-to-all-start.1) | async-done | bytes 1310752 | tf_op jit(solution)/shard_map/all_to_all | solution.py:357
  96.7 2.7 %shard_map.72 = bf16[1280,512]{1,0:T(8,128)(2,1)} custom-call(bf16[1280,512]{1,0:T(8,128)(2,1)S(1)} %bitcast.22, f32[8,384]{1,0:T(8,128)S(1)} %get-tuple-element.35.table_ref, f32[384,8]{1,0:T(8,128)S(1)} %get-tuple-element.36.columns_ref), custom_call_target="tpu_custom_call" | custom-call | tf_op jit(solution)/shard_map/pallas_call | solution.py:34
  99.4 4.9 %all-to-all-start.2 = ((bf16[32,40,512]{2,1,0:T(8,128)(2,1)}), bf16[32,40,512]{2,1,0:T(8,128)(2,1)S(1)}, u32[]{:S(2)}, u32[]{:S(2)}) async-start(bf16[32,40,512]{2,1,0:T(8,128)(2,1)} %bitcast.33), calls=%async_computation.2 | async-start | bytes 2621440 | tf_op jit(solution)/shard_map/all_to_all | solution.py:357
  104.3 9.8 %all-gather.7.cloned.1.call-done = bf16[32,160,128]{2,1,0:T(8,128)(2,1)} async-done(((bf16[4,160,128]{2,1,0:T(8,128)(2,1)}), bf16[32,160,128]{2,1,0:T(8,128)(2,1)}) %all-gather.7.cloned.1.call-update) | async-done | bytes 1310736 | tf_op jit(solution)/shard_map/all_gather | solution.py:364
  114.1 9.2 %all-to-all-done.2 = bf16[32,40,512]{2,1,0:T(8,128)(2,1)S(1)} async-done(((bf16[32,40,512]{2,1,0:T(8,128)(2,1)}), bf16[32,40,512]{2,1,0:T(8,128)(2,1)S(1)}, u32[]{:S(2)}, u32[]{:S(2)}) %all-to-all-start.2) | async-done | bytes 1310752 | tf_op jit(solution)/shard_map/all_to_all | solution.py:357
  123.3 9.8 %shard_map.73 = bf16[1280,512]{1,0:T(8,128)(2,1)} custom-call(s32[1]{0:T(128)} %bitcast.place_ref, bf16[1280,512]{1,0:T(8,128)(2,1)S(1)} %bitcast.24, bf16[2,4,512,2048]{3,2,1,0:T(8,128)(2,1)} %sites_hbm.3, bf16[8,4,160,128]{3,2,1,0:T(8,128)(2,1)} %bitcast.35), custom_call_target="tpu_custom_call" | custom-call | tf_op jit(solution)/shard_map/pallas_call | solution.py:311
  133.1 4.9 %all-to-all-start.3 = ((bf16[32,40,512]{2,1,0:T(8,128)(2,1)}), bf16[32,40,512]{2,1,0:T(8,128)(2,1)S(1)}, u32[]{:S(2)}, u32[]{:S(2)}) async-start(bf16[32,40,512]{2,1,0:T(8,128)(2,1)} %bitcast.32), calls=%async_computation.3 | async-start | bytes 2621440 | tf_op jit(solution)/shard_map/all_to_all | solution.py:357
  138.5 18.5 %all-to-all-done.3 = bf16[32,40,512]{2,1,0:T(8,128)(2,1)S(1)} async-done(((bf16[32,40,512]{2,1,0:T(8,128)(2,1)}), bf16[32,40,512]{2,1,0:T(8,128)(2,1)S(1)}, u32[]{:S(2)}, u32[]{:S(2)}) %all-to-all-start.3) | async-done | bytes 1310752 | tf_op jit(solution)/shard_map/all_to_all | solution.py:357
  157.0 1.9 %shard_map.75 = (bf16[8,384]{1,0:T(8,128)(2,1)}, bf16[384,512]{1,0:T(8,128)(2,1)}) custom-call(bf16[1280,512]{1,0:T(8,128)(2,1)S(1)} %bitcast.26, f32[384,8]{1,0:T(8,128)S(1)} %get-tuple-element.36.columns_ref, f32[384,8]{1,0:T(8,128)S(1)} %shard_map.74.probs0_ref), custom_call_target="tpu_custom_call" | custom-call | tf_op jit(solution)/shard_map/pallas_call | solution.py:34
  (22 shorter events, 3.2 us)
Async XLA Ops:
  7.2 49.3 %all-gather.5.cloned.1.call-start = ((), (), s32[]{:S(2)}) async-start(), calls=%async_computation.4 | async-start | bytes 1474560 | tf_op jit(solution)/shard_map/all_gather | solution.py:345
  7.2 1.0 copy-start
  8.3 8.9 %copy-start.1 = (bf16[2,4,4,16,512]{4,3,2,1,0:T(8,128)(2,1)S(1)}, bf16[2,4,4,16,512]{4,3,2,1,0:T(8,128)(2,1)}, u32[]{:S(2)}) copy-start(bf16[2,4,4,16,512]{4,3,2,1,0:T(8,128)(2,1)} %rest_ref.2) | copy-start | bytes 1572868
  8.4 16.0 %copy-start.2 = (bf16[384,512]{1,0:T(8,128)(2,1)S(1)}, bf16[384,512]{1,0:T(8,128)(2,1)}, u32[]{:S(2)}) copy-start(bf16[384,512]{1,0:T(8,128)(2,1)} %vec_ref) | copy-start | bytes 1179652
  8.4 16.0 %copy-start.3 = (s32[384,2]{0,1:T(2,128)S(1)}, s32[384,2]{0,1:T(2,128)}, u32[]{:S(2)}) copy-start(s32[384,2]{0,1:T(2,128)} %param.6) | copy-start | bytes 9220
  8.4 16.0 %copy-start.4 = (s32[384,2]{0,1:T(2,128)S(1)}, s32[384,2]{0,1:T(2,128)}, u32[]{:S(2)}) copy-start(s32[384,2]{0,1:T(2,128)} %param.7) | copy-start | bytes 9220
  8.4 5.9 %collective-permute-start = (bf16[160,128]{1,0:T(8,128)(2,1)S(1)}, bf16[160,128]{1,0:T(8,128)(2,1)S(1)}, u32[]{:S(2)}, u32[]{:S(2)}) collective-permute-start(bf16[160,128]{1,0:T(8,128)(2,1)S(1)} %get-tuple-element.22), channel_id=1, source_target_pairs={{0,1},{1,2},{2,3},{3,0},{4,5},{5,6},{6,7},{7,4},{8,9},{9,10},{10,1... | collective-permute-start | bytes 122888 | tf_op jit(solution)/shard_map/ppermute | solution.py:338
  10.6 4.4 %collective-permute-start.1 = (bf16[160,128]{1,0:T(8,128)(2,1)S(1)}, bf16[160,128]{1,0:T(8,128)(2,1)S(1)}, u32[]{:S(2)}, u32[]{:S(2)}) collective-permute-start(bf16[160,128]{1,0:T(8,128)(2,1)S(1)} %get-tuple-element.23), channel_id=1, source_target_pairs={{0,2},{1,3},{2,0},{3,1},{4,6},{5,7},{6,4},{7,5},{8,10},{9,11},{10,... | collective-permute-start | bytes 122888 | tf_op jit(solution)/shard_map/ppermute | solution.py:338
  13.3 3.1 %collective-permute-start.2 = (bf16[160,128]{1,0:T(8,128)(2,1)S(1)}, bf16[160,128]{1,0:T(8,128)(2,1)S(1)}, u32[]{:S(2)}, u32[]{:S(2)}) collective-permute-start(bf16[160,128]{1,0:T(8,128)(2,1)S(1)} %get-tuple-element.24), channel_id=1, source_target_pairs={{0,3},{1,0},{2,1},{3,2},{4,7},{5,4},{6,5},{7,6},{8,11},{9,8},{10,9... | collective-permute-start | bytes 122888 | tf_op jit(solution)/shard_map/ppermute | solution.py:338
  17.3 4.1 %collective-permute-start.3 = (bf16[160,128]{1,0:T(8,128)(2,1)S(1)}, bf16[160,128]{1,0:T(8,128)(2,1)S(1)}, u32[]{:S(2)}, u32[]{:S(2)}) collective-permute-start(bf16[160,128]{1,0:T(8,128)(2,1)S(1)} %get-tuple-element.27), channel_id=1, source_target_pairs={{0,1},{1,2},{2,3},{3,0},{4,5},{5,6},{6,7},{7,4},{8,9},{9,10},{10,1... | collective-permute-start | bytes 122888 | tf_op jit(solution)/shard_map/ppermute | solution.py:338
  17.4 5.0 %collective-permute-start.4 = (bf16[160,128]{1,0:T(8,128)(2,1)S(1)}, bf16[160,128]{1,0:T(8,128)(2,1)S(1)}, u32[]{:S(2)}, u32[]{:S(2)}) collective-permute-start(bf16[160,128]{1,0:T(8,128)(2,1)S(1)} %get-tuple-element.28), channel_id=1, source_target_pairs={{0,2},{1,3},{2,0},{3,1},{4,6},{5,7},{6,4},{7,5},{8,10},{9,11},{10,... | collective-permute-start | bytes 122888 | tf_op jit(solution)/shard_map/ppermute | solution.py:338
  20.5 3.1 %collective-permute-start.5 = (bf16[160,128]{1,0:T(8,128)(2,1)S(1)}, bf16[160,128]{1,0:T(8,128)(2,1)S(1)}, u32[]{:S(2)}, u32[]{:S(2)}) collective-permute-start(bf16[160,128]{1,0:T(8,128)(2,1)S(1)} %get-tuple-element.29), channel_id=1, source_target_pairs={{0,3},{1,0},{2,1},{3,2},{4,7},{5,4},{6,5},{7,6},{8,11},{9,8},{10,9... | collective-permute-start | bytes 122888 | tf_op jit(solution)/shard_map/ppermute | solution.py:338
  26.6 29.9 %all-to-all-start = ((bf16[32,40,512]{2,1,0:T(8,128)(2,1)}), bf16[32,40,512]{2,1,0:T(8,128)(2,1)S(1)}, u32[]{:S(2)}, u32[]{:S(2)}) async-start(bf16[32,40,512]{2,1,0:T(8,128)(2,1)} %bitcast.36), calls=%async_computation | async-start | bytes 2621440 | tf_op jit(solution)/shard_map/all_to_all | solution.py:357
  66.3 30.4 %all-to-all-start.1 = ((bf16[32,40,512]{2,1,0:T(8,128)(2,1)}), bf16[32,40,512]{2,1,0:T(8,128)(2,1)S(1)}, u32[]{:S(2)}, u32[]{:S(2)}) async-start(bf16[32,40,512]{2,1,0:T(8,128)(2,1)} %bitcast.31), calls=%async_computation.1 | async-start | bytes 2621440 | tf_op jit(solution)/shard_map/all_to_all | solution.py:357
  77.8 36.3 %all-gather.7.cloned.1.call-start = ((), (), s32[]{:S(2)}) async-start(), calls=%async_computation.5 | async-start | bytes 1474560 | tf_op jit(solution)/shard_map/all_gather | solution.py:364
  99.4 23.9 %all-to-all-start.2 = ((bf16[32,40,512]{2,1,0:T(8,128)(2,1)}), bf16[32,40,512]{2,1,0:T(8,128)(2,1)S(1)}, u32[]{:S(2)}, u32[]{:S(2)}) async-start(bf16[32,40,512]{2,1,0:T(8,128)(2,1)} %bitcast.33), calls=%async_computation.2 | async-start | bytes 2621440 | tf_op jit(solution)/shard_map/all_to_all | solution.py:357
  133.1 23.9 %all-to-all-start.3 = ((bf16[32,40,512]{2,1,0:T(8,128)(2,1)}), bf16[32,40,512]{2,1,0:T(8,128)(2,1)S(1)}, u32[]{:S(2)}, u32[]{:S(2)}) async-start(bf16[32,40,512]{2,1,0:T(8,128)(2,1)} %bitcast.32), calls=%async_computation.3 | async-start | bytes 2621440 | tf_op jit(solution)/shard_map/all_to_all | solution.py:357
Sparse Core Ops, SparseCore 0:
  17.2 39.1 all-gather.4
  80.4 33.6 all-gather.6
